TPU v7x, 32 devices: a whole 2x2x4 slice. The times are simulated.
32 devices in a mesh: rep: 4 (over x, core), shard: 8 (over z, y).
Axes of the slice: x: 2, y: 2, z: 4, core: 2. Of those that a mesh axis runs over, the one named last changes fastest.
Arguments:
- tokens: bfloat16 [16384, 1024], P(('rep', 'shard')), may hold values from -6 to 6
- seg_ids: int32 [16384], P('rep'), may hold values from 0 to 63, never falling along the last dimension, each value on 1 to 2048 neighbouring positions
- w_qkv: bfloat16 [1024, 3072], P('shard'), may hold values from -0.1875 to 0.1875
- w_out: bfloat16 [1024, 1024], P('shard'), may hold values from -0.75 to 0.75
- w_in: bfloat16 [1024, 5248], P('shard'), may hold values from -0.1875 to 0.1875
- w_down: bfloat16 [2624, 1024], P('shard'), may hold values from -0.125 to 0.125
- attn_gain: bfloat16 [1024], P('shard'), may hold values from 0.5 to 1.5
- ffn_gain: bfloat16 [1024], P('shard'), may hold values from 0.5 to 1.5
- cotangent: bfloat16 [16384, 1024], P(('rep', 'shard')), may hold values from -6 to 6
Outputs:
- layer_out: bfloat16 [16384, 1024], P(('rep', 'shard'))
- grad_tokens: bfloat16 [16384, 1024], P(('rep', 'shard'))
- grad_attn_gain: float32 [1024], P('shard')
- grad_ffn_gain: float32 [1024], P('shard')
- grad_qkv: float32 [1024, 3072], P('shard')
- grad_out: float32 [1024, 1024], P('shard')
- grad_in: float32 [1024, 5248], P('shard')
- grad_down: float32 [2624, 1024], P('shard')
Inputs may be any that keep to these rules, and one draw needn't show every extreme that they name: `seg_ids`: ids never fall along the tokens; a document may run across sequence ends, attention stays within both.
All inputs are finite; a program needn't handle non-finite values.
Results may differ from a plain program's by a relative error of at most 0.02.
Values may be sent and summed in bfloat16 or wider, within the bound.
No kernel may reach another device: no remote copies, remote signals or barrier semaphores. Data moves between devices by JAX's collectives and lax.ppermute only.
A program may use at most 256 MiB of HBM per device.

v0:
```python
import jax
import jax.numpy as jnp
from jax import lax
from jax.sharding import PartitionSpec as P

HEAD_DIM = 64
LOG_SPAN = 3


THETA = 160000.0
EPS = 1e-05
SCALE = 0.125
MASKED = -1e30


def swapped(shard, axis, stride):
    return lax.ppermute(shard, axis, [(i, i ^ 1 << stride) for i in range(lax.axis_size(axis))])


def norm_rows(values, gain_vec):
    centered = values - jnp.mean(values, axis=-1, keepdims=True)
    variance = jnp.mean(centered * centered, axis=-1, keepdims=True)
    return centered * lax.rsqrt(variance + EPS) * gain_vec


def rotate(values, positions):
    half_size = values.shape[-1] // 2
    frequency = THETA ** (-(jnp.arange(half_size, dtype=jnp.float32) * 2.0 / values.shape[-1]))
    angles = positions.astype(jnp.float32)[:, None] * frequency[None, :]
    cosine = jnp.cos(angles)[:, None, :]
    sine_part = jnp.sin(angles)[:, None, :]
    first_half = values[..., :half_size]
    second_half = values[..., half_size:]
    return jnp.concatenate(
        [
            first_half * cosine - second_half * sine_part,
            second_half * cosine + first_half * sine_part,
        ],
        axis=-1,
    )


def gated_units(pre_act):
    units = pre_act.shape[1] // 2
    return jax.nn.gelu(pre_act[:, :units], approximate=False) * pre_act[:, units:]


def split_heads(matrix, head_size):
    return jnp.transpose(matrix.reshape(matrix.shape[0], -1, head_size), (1, 0, 2))


def merge_heads(stacked):
    return jnp.transpose(stacked, (1, 0, 2)).reshape(stacked.shape[1], -1)


def local(tokens, seg_ids, w_qkv, w_out, w_in, w_down, attn_gain, ffn_gain, cotangent):
    rows_here = tokens.shape[0]
    model_width = tokens.shape[1]
    head_size = HEAD_DIM
    span_size = 2**LOG_SPAN
    position = lax.axis_index("shard")
    my_offset = position % span_size
    weights = (
        lax.all_gather(w_qkv, "shard", axis=0, tiled=True),
        lax.all_gather(w_out, "shard", axis=0, tiled=True),
        lax.all_gather(w_in, "shard", axis=0, tiled=True),
        lax.all_gather(w_down, "shard", axis=0, tiled=True),
        lax.all_gather(attn_gain, "shard", axis=0, tiled=True),
        lax.all_gather(ffn_gain, "shard", axis=0, tiled=True),
    )
    full_qkv, full_out, full_in, full_down, gain_first, gain_second = weights
    gain_one = gain_first.astype(jnp.float32)
    gain_two = gain_second.astype(jnp.float32)
    positions = my_offset * rows_here + jnp.arange(rows_here, dtype=jnp.int32)
    query_seg = lax.dynamic_slice_in_dim(seg_ids, position * rows_here, rows_here)
    key_seg = lax.dynamic_slice_in_dim(
        seg_ids, (position - my_offset) * rows_here, span_size * rows_here
    )
    same_doc = query_seg[:, None] == key_seg[None, :]
    resid_in = tokens.astype(jnp.float32)
    normed_one = norm_rows(resid_in, gain_one).astype(jnp.bfloat16)
    projected = jnp.dot(normed_one, full_qkv, preferred_element_type=jnp.float32)
    query_raw = projected[:, :model_width].reshape(rows_here, -1, head_size)
    key_raw = projected[:, model_width : 2 * model_width].reshape(rows_here, -1, head_size)
    query_low = rotate(query_raw, positions).astype(jnp.bfloat16).reshape(rows_here, model_width)
    key_low = rotate(key_raw, positions).astype(jnp.bfloat16).reshape(rows_here, model_width)
    value_low = projected[:, 2 * model_width :].astype(jnp.bfloat16)
    joined = jnp.stack([key_low, value_low], 0)
    for bit_index in range(LOG_SPAN):
        partner = swapped(joined, "shard", bit_index)
        is_upper = my_offset // 2**bit_index % 2 == 1
        joined = jnp.where(
            is_upper, jnp.concatenate([partner, joined], 1), jnp.concatenate([joined, partner], 1)
        )
    query_heads = split_heads(query_low, head_size)
    key_heads = split_heads(joined[0], head_size)
    value_heads = split_heads(joined[1], head_size)

    def head_forward(operands):
        query_h, key_h, value_h = operands
        scores = jnp.einsum("qe,ke->qk", query_h, key_h, preferred_element_type=jnp.float32) * SCALE
        scores = jnp.where(same_doc, scores, MASKED)
        largest = jnp.max(scores, axis=1, keepdims=True)
        exponent = jnp.exp(scores - largest)
        row_total = jnp.sum(exponent, axis=1, keepdims=True)
        probs_low = (exponent / row_total).astype(jnp.bfloat16)
        head_out = jnp.dot(probs_low, value_h, preferred_element_type=jnp.float32)
        return (head_out, largest[:, 0] + jnp.log(row_total[:, 0]))

    heads_out, log_totals = lax.map(head_forward, (query_heads, key_heads, value_heads))
    attn_low = merge_heads(heads_out).astype(jnp.bfloat16)
    resid_mid = resid_in + jnp.dot(attn_low, full_out, preferred_element_type=jnp.float32)
    normed_two = norm_rows(resid_mid, gain_two).astype(jnp.bfloat16)
    pre_act = jnp.dot(normed_two, full_in, preferred_element_type=jnp.float32)
    units_low = gated_units(pre_act).astype(jnp.bfloat16)
    layer_out = (
        resid_mid + jnp.dot(units_low, full_down, preferred_element_type=jnp.float32)
    ).astype(jnp.bfloat16)
    back_weights = (
        lax.all_gather(w_qkv, "shard", axis=0, tiled=True),
        lax.all_gather(w_out, "shard", axis=0, tiled=True),
        lax.all_gather(w_in, "shard", axis=0, tiled=True),
        lax.all_gather(w_down, "shard", axis=0, tiled=True),
        lax.all_gather(attn_gain, "shard", axis=0, tiled=True),
        lax.all_gather(ffn_gain, "shard", axis=0, tiled=True),
    )
    back_qkv, back_out, back_in, back_down, back_gain_first, back_gain_second = back_weights
    back_gain_one = back_gain_first.astype(jnp.float32)
    back_gain_two = back_gain_second.astype(jnp.float32)
    grad_resid_out = cotangent.astype(jnp.float32)
    grad_down = jnp.einsum("tf,td->fd", units_low, cotangent, preferred_element_type=jnp.float32)
    grad_units = jnp.einsum("td,fd->tf", cotangent, back_down, preferred_element_type=jnp.float32)
    grad_units_low = grad_units.astype(jnp.bfloat16)
    unused_units, pull_gate = jax.vjp(gated_units, pre_act)
    grad_pre = pull_gate(grad_units_low.astype(jnp.float32))[0].astype(jnp.bfloat16)
    grad_in = jnp.einsum("td,tf->df", normed_two, grad_pre, preferred_element_type=jnp.float32)
    grad_normed_two = jnp.einsum(
        "tf,df->td", grad_pre, back_in, preferred_element_type=jnp.float32
    ).astype(jnp.bfloat16)
    unused_norm, pull_norm_two = jax.vjp(norm_rows, resid_mid, back_gain_two)
    grad_mid_norm, grad_gain_two = pull_norm_two(grad_normed_two.astype(jnp.float32))
    grad_resid = grad_resid_out + grad_mid_norm
    grad_branch_low = grad_resid.astype(jnp.bfloat16)
    grad_out = jnp.einsum(
        "td,te->de", attn_low, grad_branch_low, preferred_element_type=jnp.float32
    )
    grad_attn = jnp.einsum(
        "te,de->td", grad_branch_low, back_out, preferred_element_type=jnp.float32
    ).astype(jnp.bfloat16)
    grad_heads = split_heads(grad_attn, head_size)

    def head_backward(operands):
        query_h, key_h, value_h, grad_h, lse_h = operands
        scores = jnp.einsum("qe,ke->qk", query_h, key_h, preferred_element_type=jnp.float32) * SCALE
        scores = jnp.where(same_doc, scores, MASKED)
        probs = jnp.exp(scores - lse_h[:, None])
        probs_low = probs.astype(jnp.bfloat16)
        grad_value_h = jnp.einsum(
            "qk,qe->ke", probs_low, grad_h, preferred_element_type=jnp.float32
        )
        grad_probs = jnp.einsum("qe,ke->qk", grad_h, value_h, preferred_element_type=jnp.float32)
        inner_sum = jnp.sum(probs * grad_probs, axis=1, keepdims=True)
        grad_scores = (probs * (grad_probs - inner_sum)).astype(jnp.bfloat16)
        grad_query_h = (
            jnp.einsum("qk,ke->qe", grad_scores, key_h, preferred_element_type=jnp.float32) * SCALE
        )
        grad_key_h = (
            jnp.einsum("qk,qe->ke", grad_scores, query_h, preferred_element_type=jnp.float32)
            * SCALE
        )
        return (grad_query_h, grad_key_h, grad_value_h)

    grad_query_heads, grad_key_heads, grad_value_heads = lax.map(
        head_backward, (query_heads, key_heads, value_heads, grad_heads, log_totals)
    )
    partial_sums = jnp.stack([merge_heads(grad_key_heads), merge_heads(grad_value_heads)], 0)
    for bit_index in reversed(range(LOG_SPAN)):
        half_rows = partial_sums.shape[1] // 2
        is_upper = my_offset // 2**bit_index % 2 == 1
        lower_part = partial_sums[:, :half_rows]
        upper_part = partial_sums[:, half_rows:]
        retained = jnp.where(is_upper, upper_part, lower_part)
        outgoing = jnp.where(is_upper, lower_part, upper_part)
        partial_sums = retained + swapped(outgoing.astype(jnp.bfloat16), "shard", bit_index).astype(
            outgoing.dtype
        )
    unused_rot, pull_rotate = jax.vjp(lambda values: rotate(values, positions), query_raw)
    grad_query_raw = pull_rotate(jnp.transpose(grad_query_heads, (1, 0, 2)))[0]
    grad_key_raw = pull_rotate(partial_sums[0].reshape(rows_here, -1, head_size))[0]
    grad_proj = jnp.concatenate(
        [
            grad_query_raw.reshape(rows_here, model_width),
            grad_key_raw.reshape(rows_here, model_width),
            partial_sums[1],
        ],
        1,
    ).astype(jnp.bfloat16)
    grad_qkv = jnp.einsum("td,tf->df", normed_one, grad_proj, preferred_element_type=jnp.float32)
    grad_normed_one = jnp.einsum(
        "tf,df->td", grad_proj, back_qkv, preferred_element_type=jnp.float32
    ).astype(jnp.bfloat16)
    unused_first, pull_norm_one = jax.vjp(norm_rows, resid_in, back_gain_one)
    grad_in_norm, grad_gain_one = pull_norm_one(grad_normed_one.astype(jnp.float32))
    grad_tokens = (grad_resid + grad_in_norm).astype(jnp.bfloat16)
    shares = (
        lax.psum_scatter(grad_qkv, "shard", scatter_dimension=0, tiled=True),
        lax.psum_scatter(grad_out, "shard", scatter_dimension=0, tiled=True),
        lax.psum_scatter(grad_in, "shard", scatter_dimension=0, tiled=True),
        lax.psum_scatter(grad_down, "shard", scatter_dimension=0, tiled=True),
        lax.psum_scatter(grad_gain_one, "shard", scatter_dimension=0, tiled=True),
        lax.psum_scatter(grad_gain_two, "shard", scatter_dimension=0, tiled=True),
    )
    totals = (
        lax.psum(shares[0].astype(jnp.bfloat16), "rep").astype(jnp.float32),
        lax.psum(shares[1].astype(jnp.bfloat16), "rep").astype(jnp.float32),
        lax.psum(shares[2].astype(jnp.bfloat16), "rep").astype(jnp.float32),
        lax.psum(shares[3].astype(jnp.bfloat16), "rep").astype(jnp.float32),
        lax.psum(shares[4].astype(jnp.bfloat16), "rep").astype(jnp.float32),
        lax.psum(shares[5].astype(jnp.bfloat16), "rep").astype(jnp.float32),
    )
    return (
        layer_out,
        grad_tokens,
        totals[4],
        totals[5],
        totals[0],
        totals[1],
        totals[2],
        totals[3],
    )


def solution(mesh):
    in_specs = (
        P(("rep", "shard"), None),
        P("rep"),
        P("shard", None),
        P("shard", None),
        P("shard", None),
        P("shard", None),
        P("shard"),
        P("shard"),
        P(("rep", "shard"), None),
    )
    out_specs = (
        P(("rep", "shard"), None),
        P(("rep", "shard"), None),
        P("shard"),
        P("shard"),
        P("shard", None),
        P("shard", None),
        P("shard", None),
        P("shard", None),
    )
    return jax.shard_map(local, mesh=mesh, in_specs=in_specs, out_specs=out_specs, check_vma=False)
```

profile of v0, /device:TPU:0, one launch (start us, length us, event | category | flops | bytes accessed | tf_op | source)
XLA Modules:
  0.0 2803.2 jit_solution(11736617701700225761)
XLA Ops:
  10.9 22.8 all-gather
  36.4 75.3 %all-gather.7.cloned.1.call-done = bf16[1024,3072]{1,0:T(8,128)(2,1)} async-done(((bf16[128,3072]{1,0:T(8,128)(2,1)}), bf16[1024,3072]{1,0:T(8,128)(2,1)}) %all-gather.7.cloned.1.call-update) | async-done | bytes 6291472 | tf_op jit(solution)/shard_map/all_gather | solution.py:64
  133.1 64.7 %collective-permute-done = bf16[2,512,1024]{2,1,0:T(8,128)(2,1)} collective-permute-done((bf16[2,512,1024]{2,1,0:T(8,128)(2,1)}, bf16[2,512,1024]{2,1,0:T(8,128)(2,1)}, u32[]{:S(2)}, u32[]{:S(2)}) %collective-permute-start) | collective-permute-done | bytes 2097184 | tf_op jit(solution)/shard_map/ppermute | solution.py:17
  202.7 202.1 %collective-permute-done.1 = bf16[2,1024,1024]{2,1,0:T(8,128)(2,1)} collective-permute-done((bf16[2,1024,1024]{2,1,0:T(8,128)(2,1)}, bf16[2,1024,1024]{2,1,0:T(8,128)(2,1)}, u32[]{:S(2)}, u32[]{:S(2)}) %collective-permute-start.1) | collective-permute-done | bytes 4194336 | tf_op jit(solution)/shard_map/ppermute | solution.py:17
  404.8 9.9 maximum_select_fusion.1
  415.3 206.0 %all-gather.1 = bf16[8,1,128]{2,1,0:T(2,128)(2,1)S(1)} all-gather(bf16[1,1,128]{2,1,0:T(2,128)(2,1)S(1)} %bitcast.193), channel_id=1, replica_groups=mesh['rep'=4,'shard'=8] {'shard'}, dimensions={0}, use_global_device_ids=true | all-gather | bytes 2304 | tf_op jit(solution)/shard_map/all_gather | solution.py:69
  623.7 218.7 %collective-permute-done.2 = bf16[2,2048,1024]{2,1,0:T(8,128)(2,1)} collective-permute-done((bf16[2,2048,1024]{2,1,0:T(8,128)(2,1)}, bf16[2,2048,1024]{2,1,0:T(8,128)(2,1)}, u32[]{:S(2)}, u32[]{:S(2)}) %collective-permute-start.2) | collective-permute-done | bytes 8388640 | tf_op jit(solution)/shard_map/ppermute | solution.py:17
  842.4 13.3 maximum_select_fusion
  862.0 11.9 copy.46
  873.9 15.5 copy.49
  889.4 11.9 copy.45
  901.3 15.6 copy.48
  916.9 125.4 %while.30 = (s32[]{:T(128)}, bf16[16,512,64]{1,2,0:T(8,128)(2,1)}, f32[16,512]{1,0:T(8,128)S(1)}, bf16[16,512,64]{2,1,0:T(8,128)(2,1)S(1)}, bf16[16,4096,64]{2,1...) while((s32[]{:T(128)}, bf16[16,512,64]{1,2,0:T(8,128)(2,1)}, ...), condition=%wide.region_5.6_spmd.clone.clone, body=%wide.region_2.5_spmd.clone.sunk.clone | while | flops 555744768 | bytes 27566176 | solution.py:110
  1047.4 13.1 fusion.79
  1060.5 18.8 convert_multiply_fusion.1
  1084.5 13.5 fusion.60
  1111.0 7.4 fusion.87
  1118.6 485.8 %while.31 = (s32[]{:T(128)}, f32[16,512,64]{1,2,0:T(8,128)}, f32[16,4096,64]{1,2,0:T(8,128)}, f32[16,4096,64]{1,2,0:T(8,128)}, bf16[16,512,64]{2,1,0:T(8,128)(2,...) while((s32[]{:T(128)}, f32[16,512,64]{1,2,0:T(8,128)}, ...), condition=%wide.region_12.13_spmd.clone.clone, body=%wide.region_10.12_spmd.clone.sunk.clone | while | flops 1363443200 | bytes 102270096 | solution.py:173
  1121.2 8.4 multiply_reduce_fusion.4
  1129.6 8.1 multiply_convert_fusion.7
  1151.7 8.4 multiply_reduce_fusion.4
  1160.1 8.0 multiply_convert_fusion.7
  1182.0 8.4 multiply_reduce_fusion.4
  1190.3 8.1 multiply_convert_fusion.7
  1212.3 8.4 multiply_reduce_fusion.4
  1220.6 8.0 multiply_convert_fusion.7
  1242.6 8.4 multiply_reduce_fusion.4
  1250.9 8.5 multiply_convert_fusion.7
  1273.5 8.4 multiply_reduce_fusion.4
  1281.9 8.0 multiply_convert_fusion.7
  1303.9 8.4 multiply_reduce_fusion.4
  1312.3 8.6 multiply_convert_fusion.7
  1334.8 8.7 multiply_reduce_fusion.4
  1343.4 7.9 multiply_convert_fusion.7
  1365.3 8.4 multiply_reduce_fusion.4
  1373.7 8.0 multiply_convert_fusion.7
  1395.7 8.4 multiply_reduce_fusion.4
  1404.0 7.9 multiply_convert_fusion.7
  1425.9 8.4 multiply_reduce_fusion.4
  1434.2 7.9 multiply_convert_fusion.7
  1456.0 8.4 multiply_reduce_fusion.4
  1464.4 7.9 multiply_convert_fusion.7
  1486.2 8.4 multiply_reduce_fusion.4
  1494.6 7.9 multiply_convert_fusion.7
  1516.5 8.4 multiply_reduce_fusion.4
  1524.8 7.9 multiply_convert_fusion.7
  1546.7 8.4 multiply_reduce_fusion.4
  1555.0 7.9 multiply_convert_fusion.7
  1576.8 8.4 multiply_reduce_fusion.4
  1585.2 7.9 multiply_convert_fusion.7
  1604.4 11.5 select_convert_fusion
  1615.9 13.0 collective-permute-start.3
  1628.9 356.4 %collective-permute-done.3 = bf16[2,2048,1024]{1,2,0:T(8,128)(2,1)S(1)} collective-permute-done((bf16[2,2048,1024]{1,2,0:T(8,128)(2,1)S(1)}, bf16[2,2048,1024]{1,2,0:T(8,128)(2,1)S(1)}, u32[]{:S(2)}, u32[]{:S(2)}) %collective-permute-start.3) | collective-permute-done | bytes 8388640 | tf_op jit(solution)/shard_map/ppermute | solution.py:17
  1985.3 12.6 convert_add_fusion
  1998.7 91.6 %collective-permute-done.4 = bf16[2,1024,1024]{1,2,0:T(8,128)(2,1)} collective-permute-done((bf16[2,1024,1024]{1,2,0:T(8,128)(2,1)S(1)}, bf16[2,1024,1024]{1,2,0:T(8,128)(2,1)}, u32[]{:S(2)}, u32[]{:S(2)}) %collective-permute-start.4) | collective-permute-done | bytes 4194336 | tf_op jit(solution)/shard_map/ppermute | solution.py:17
  2097.1 44.5 %collective-permute-done.5 = bf16[2,512,1024]{1,2,0:T(8,128)(2,1)S(1)} collective-permute-done((bf16[2,512,1024]{1,2,0:T(8,128)(2,1)S(1)}, bf16[2,512,1024]{1,2,0:T(8,128)(2,1)S(1)}, u32[]{:S(2)}, u32[]{:S(2)}) %collective-permute-start.5) | collective-permute-done | bytes 2097184 | tf_op jit(solution)/shard_map/ppermute | solution.py:17
  2147.4 9.7 fusion.66
  2158.7 14.7 fusion.69
  2175.3 7.5 add_convert_fusion.4
  2186.9 178.2 %reduce-scatter.5.cloned.1.call-done = f32[128,3072]{1,0:T(8,128)} async-done(((f32[1024,3072]{1,0:T(8,128)}), f32[128,3072]{1,0:T(8,128)}) %reduce-scatter.5.cloned.1.call-update) | async-done | bytes 1572880 | tf_op jit(solution)/shard_map/reduce_scatter | solution.py:206
  2367.4 350.7 %reduce-scatter.9.cloned.1.call-done = f32[128,5248]{1,0:T(8,128)} async-done(((f32[1024,5248]{1,0:T(8,128)}), f32[128,5248]{1,0:T(8,128)}) %reduce-scatter.9.cloned.1.call-update) | async-done | bytes 2686992 | tf_op jit(solution)/shard_map/reduce_scatter | solution.py:208
  2721.1 7.6 fusion.63
  2731.0 19.7 all-reduce.8
  2760.6 27.3 all-reduce.13.cloned.1.call-done
  (372 shorter events, 458.4 us)
Async XLA Ops:
  7.2 104.5 %all-gather.7.cloned.1.call-start = ((), (), s32[]{:S(2)}) async-start(), calls=%async_computation.4 | async-start | bytes 7077888 | tf_op jit(solution)/shard_map/all_gather | solution.py:64
  7.9 1034.5 %all-gather.9.cloned.1.call-start = ((), (), s32[]{:S(2)}) async-start(), calls=%async_computation.5 | async-start | bytes 2359296 | tf_op jit(solution)/shard_map/all_gather | solution.py:65
  8.6 1038.7 %all-gather.11.cloned.1.call-start = ((), (), s32[]{:S(2)}) async-start(), calls=%async_computation.6 | async-start | bytes 12091392 | tf_op jit(solution)/shard_map/all_gather | solution.py:66
  9.4 1051.1 %all-gather.13.cloned.1.call-start = ((), (), s32[]{:S(2)}) async-start(), calls=%async_computation.7 | async-start | bytes 6045696 | tf_op jit(solution)/shard_map/all_gather | solution.py:67
  10.9 106.8 %copy-start.27 = (f32[512]{0:T(512)}, f32[512]{0:T(512)S(1)}, u32[]{:S(2)}) copy-start(f32[512]{0:T(512)S(1)} %broadcast_multiply_fusion.1) | copy-start | bytes 6148
  33.8 83.9 %copy-start.25 = (f32[8,1,128]{2,1,0:T(1,128)}, f32[8,1,128]{2,1,0:T(1,128)S(1)}, u32[]{:S(2)}) copy-start(f32[8,1,128]{2,1,0:T(1,128)S(1)} %convert_element_type.192) | copy-start | bytes 12292
  36.0 81.7 %copy-start.31 = (f32[512]{0:T(512)}, f32[512]{0:T(512)S(1)}, u32[]{:S(2)}) copy-start(f32[512]{0:T(512)S(1)} %fusion.70) | copy-start | bytes 6148
  36.3 90.1 %copy-start.20 = (f32[512,32]{0,1:T(8,128)}, f32[512,32]{0,1:T(8,128)S(1)}, u32[]{:S(2)}) copy-start(f32[512,32]{0,1:T(8,128)S(1)} %get-tuple-element.284) | copy-start | bytes 196612
  36.3 90.1 %copy-start.22 = (f32[512,32]{0,1:T(8,128)}, f32[512,32]{0,1:T(8,128)S(1)}, u32[]{:S(2)}) copy-start(f32[512,32]{0,1:T(8,128)S(1)} %get-tuple-element.285) | copy-start | bytes 196612
  117.7 3.9 copy-start.9
  132.5 65.3 %collective-permute-start = (bf16[2,512,1024]{2,1,0:T(8,128)(2,1)}, bf16[2,512,1024]{2,1,0:T(8,128)(2,1)}, u32[]{:S(2)}, u32[]{:S(2)}) collective-permute-start(bf16[2,512,1024]{2,1,0:T(8,128)(2,1)} %pad_maximum_fusion.2), channel_id=1, source_target_pairs={{0,1},{1,0},{2,3},{3,2},{4,5},{5,4},{6,7},{7,6},{8,9},{9,8},{10,11... | collective-permute-start | bytes 6291464 | tf_op jit(solution)/shard_map/ppermute | solution.py:17
  202.7 202.1 %collective-permute-start.1 = (bf16[2,1024,1024]{2,1,0:T(8,128)(2,1)}, bf16[2,1024,1024]{2,1,0:T(8,128)(2,1)}, u32[]{:S(2)}, u32[]{:S(2)}) collective-permute-start(bf16[2,1024,1024]{2,1,0:T(8,128)(2,1)} %maximum_select_fusion.2), channel_id=1, source_target_pairs={{0,2},{1,3},{2,0},{3,1},{4,6},{5,7},{6,4},{7,5},{8,10},{9,11},{10,... | collective-permute-start | bytes 12582920 | tf_op jit(solution)/shard_map/ppermute | solution.py:17
  202.7 212.6 %copy-start.42 = (bf16[128]{0:T(256)(128)(2,1)S(1)}, bf16[128]{0:T(256)(128)(2,1)}, u32[]{:S(2)}) copy-start(bf16[128]{0:T(256)(128)(2,1)} %param.20) | copy-start | bytes 772
  202.7 418.6 %copy-start.24 = (s32[4096]{0:T(1024)S(1)}, s32[4096]{0:T(1024)}, u32[]{:S(2)}) copy-start(s32[4096]{0:T(1024)} %param.14) | copy-start | bytes 49156
  414.7 427.7 %collective-permute-start.2 = (bf16[2,2048,1024]{2,1,0:T(8,128)(2,1)}, bf16[2,2048,1024]{2,1,0:T(8,128)(2,1)}, u32[]{:S(2)}, u32[]{:S(2)}) collective-permute-start(bf16[2,2048,1024]{2,1,0:T(8,128)(2,1)} %maximum_select_fusion.1), channel_id=1, source_target_pairs={{0,4},{1,5},{2,6},{3,7},{4,0},{5,1},{6,2},{7,3},{8,12},{9,13},{10,... | collective-permute-start | bytes 25165832 | tf_op jit(solution)/shard_map/ppermute | solution.py:17
  415.2 1767.6 %reduce-scatter.7.cloned.1.call-start = ((), (), s32[]{:S(2)}) async-start(), calls=%async_computation.9 | async-start | bytes 4718592 | tf_op jit(solution)/shard_map/reduce_scatter | solution.py:207
  621.3 476.6 %copy-start.37 = (f32[8,1,128]{2,1,0:T(1,128)}, f32[8,1,128]{2,1,0:T(1,128)S(1)}, u32[]{:S(2)}) copy-start(f32[8,1,128]{2,1,0:T(1,128)S(1)} %convert_element_type.193) | copy-start | bytes 12292
  916.9 126.8 %copy-start.1 = (bf16[512,1024]{1,0:T(8,128)(2,1)S(1)}, bf16[512,1024]{1,0:T(8,128)(2,1)}, u32[]{:S(2)}) copy-start(bf16[512,1024]{1,0:T(8,128)(2,1)} %param.13) | copy-start | bytes 3145732
  1046.9 51.0 %copy-start.3 = (f32[512,1024]{1,0:T(8,128)}, f32[512,1024]{1,0:T(8,128)S(1)}, u32[]{:S(2)}) copy-start(f32[512,1024]{1,0:T(8,128)S(1)} %get-tuple-element.287) | copy-start | bytes 6291460
  1047.0 51.0 %copy-start.35 = (f32[512]{0:T(512)}, f32[512]{0:T(512)S(1)}, u32[]{:S(2)}) copy-start(f32[512]{0:T(512)S(1)} %broadcast_multiply_fusion) | copy-start | bytes 6148
  1047.3 50.7 %copy-start.39 = (f32[512]{0:T(512)}, f32[512]{0:T(512)S(1)}, u32[]{:S(2)}) copy-start(f32[512]{0:T(512)S(1)} %fusion.71) | copy-start | bytes 6148
  1047.4 13.1 copy-start.11
  1060.5 18.8 copy-start.7
  1097.9 4.7 copy-start.12
  1100.0 5.8 copy-start.29
  1102.7 3.3 copy-start.13
  1105.9 1078.7 %reduce-scatter.11.cloned.1.call-start = ((), (), s32[]{:S(2)}) async-start(), calls=%async_computation.11 | async-start | bytes 12091392 | tf_op jit(solution)/shard_map/reduce_scatter | solution.py:209
  1118.4 1246.6 %reduce-scatter.5.cloned.1.call-start = ((), (), s32[]{:S(2)}) async-start(), calls=%async_computation.8 | async-start | bytes 14155776 | tf_op jit(solution)/shard_map/reduce_scatter | solution.py:206
  1121.2 8.4 copy-start
  1151.7 8.4 copy-start
  1182.0 8.4 copy-start
  1212.3 8.4 copy-start
  1242.6 8.4 copy-start
  1273.5 8.4 copy-start
  1303.9 8.4 copy-start
  1334.7 8.7 copy-start
  1365.3 8.4 copy-start
  1395.6 8.4 copy-start
  1425.9 8.4 copy-start
  1456.0 8.4 copy-start
  1486.2 8.4 copy-start
  1516.4 8.4 copy-start
  1546.6 8.4 copy-start
  1576.8 8.4 copy-start
  1615.9 369.3 %collective-permute-start.3 = (bf16[2,2048,1024]{1,2,0:T(8,128)(2,1)S(1)}, bf16[2,2048,1024]{1,2,0:T(8,128)(2,1)S(1)}, u32[]{:S(2)}, u32[]{:S(2)}) collective-permute-start(bf16[2,2048,1024]{1,2,0:T(8,128)(2,1)S(1)} %select_convert_fusion), channel_id=1, source_target_pairs={{0,4},{1,5},{2,6},{3,7},{4,0},{5,1},{6,2},{7,3},{8,12},{9,13},{10,... | collective-permute-start | bytes 25165832 | tf_op jit(solution)/shard_map/ppermute | solution.py:17
  1998.7 91.7 %collective-permute-start.4 = (bf16[2,1024,1024]{1,2,0:T(8,128)(2,1)S(1)}, bf16[2,1024,1024]{1,2,0:T(8,128)(2,1)}, u32[]{:S(2)}, u32[]{:S(2)}) collective-permute-start(bf16[2,1024,1024]{1,2,0:T(8,128)(2,1)S(1)} %select_convert_fusion.1), channel_id=1, source_target_pairs={{0,2},{1,3},{2,0},{3,1},{4,6},{5,7},{6,4},{7,5},{8,10},{9,11},{10,... | collective-permute-start | bytes 12582920 | tf_op jit(solution)/shard_map/ppermute | solution.py:17
  2095.8 47.2 %copy-start.21 = (f32[512,32]{0,1:T(8,128)S(1)}, f32[512,32]{0,1:T(8,128)}, u32[]{:S(2)}) copy-start(f32[512,32]{0,1:T(8,128)} %copy-done.20) | copy-start | bytes 196612
  2095.8 47.2 %copy-start.23 = (f32[512,32]{0,1:T(8,128)S(1)}, f32[512,32]{0,1:T(8,128)}, u32[]{:S(2)}) copy-start(f32[512,32]{0,1:T(8,128)} %copy-done.22) | copy-start | bytes 196612
  2095.8 45.8 %collective-permute-start.5 = (bf16[2,512,1024]{1,2,0:T(8,128)(2,1)S(1)}, bf16[2,512,1024]{1,2,0:T(8,128)(2,1)S(1)}, u32[]{:S(2)}, u32[]{:S(2)}) collective-permute-start(bf16[2,512,1024]{1,2,0:T(8,128)(2,1)S(1)} %select_convert_fusion.2), channel_id=1, source_target_pairs={{0,1},{1,0},{2,3},{3,2},{4,5},{5,4},{6,7},{7,6},{8,9},{9,8},{10,11... | collective-permute-start | bytes 6291464 | tf_op jit(solution)/shard_map/ppermute | solution.py:17
  2142.8 1.6 copy-start.14
  2145.4 2.0 copy-start.2
  2145.4 2.0 copy-start.26
  2145.4 2.0 copy-start.28
  2145.4 2.0 copy-start.32
  2157.1 1.6 copy-start.36
  2157.1 1.6 copy-start.38
  2157.1 1.6 copy-start.40
  2157.1 561.0 %reduce-scatter.9.cloned.1.call-start = ((), (), s32[]{:S(2)}) async-start(), calls=%async_computation.10 | async-start | bytes 24182784 | tf_op jit(solution)/shard_map/reduce_scatter | solution.py:208
  2173.5 614.5 %all-reduce.13.cloned.1.call-start = ((), (), s32[]{:S(2)}) async-start(), calls=%async_computation.12 | async-start | bytes 6127616 | tf_op jit(solution)/shard_map/psum | solution.py:214
  2721.1 7.7 copy-start.34
  2721.1 9.9 copy-start.41
  2721.1 36.4 %copy-start.6 = (f32[512,1024]{1,0:T(8,128)S(1)}, f32[512,1024]{1,0:T(8,128)}, u32[]{:S(2)}) copy-start(f32[512,1024]{1,0:T(8,128)} %copy-done.5) | copy-start | bytes 6291460
  2721.1 36.4 %copy-start.30 = (f32[512]{0:T(512)S(1)}, f32[512]{0:T(512)}, u32[]{:S(2)}) copy-start(f32[512]{0:T(512)} %copy-done.29) | copy-start | bytes 6148
  2787.9 6.6 copy-start.15
  (10 other events, 11.2 us)
Sparse Core Ops, SparseCore 0:
  10.2 101.4 all-gather.6
  113.7 58.8 all-gather.8
  174.8 228.0 all-gather.10
  415.3 288.3 all-gather.12
  1106.0 98.1 reduce-scatter.6
  1207.7 181.5 reduce-scatter.10
  2157.3 207.7 reduce-scatter.4
  2368.9 349.1 reduce-scatter.8
  2721.3 66.5 all-reduce.12
where the time goes:
time: 2810 us; the launch traced here: 2800 us
  waiting for transfers between devices  1610 us (57%)
  matrix products  569 us (20%)
  blocking collectives  254 us (9%)
  other arithmetic  250 us (9%)
  local copies, waits for them, and re-layouts  86.5 us (3%)
    ppermute x6, waiting for transfers between devices, swapped(): lax.ppermute(shard, axis, [(i, i ^ 1 << stride) for i in range(lax.axis_s...  978 us
    reduce_scatter x1, waiting for transfers between devices, local(): lax.psum_scatter(grad_in, 'shard', scatter_dimension=0, tiled=True)  351 us
    all_gather x1, blocking collectives, local(): lax.all_gather(ffn_gain, 'shard', axis=0, tiled=True)  206 us
    reduce_scatter x1, waiting for transfers between devices, local(): lax.psum_scatter(grad_qkv, 'shard', scatter_dimension=0, tiled=True)  178 us
    dot_general x16, matrix products, head_backward(): jnp.einsum('qe,ke->qk', query_h, key_h, preferred_element_type=jnp.float32)  134 us
    convert_element_type x16, other arithmetic, head_backward(): grad_scores = (probs * (grad_probs - inner_sum)).astype(jnp.bfloat16)  129 us
    dot_general x16, matrix products, head_backward(): jnp.einsum('qk,qe->ke', probs_low, grad_h, preferred_element_type=jnp.flo...  84.6 us
    all_gather x1, waiting for transfers between devices, local(): lax.all_gather(w_qkv, 'shard', axis=0, tiled=True)  75.3 us
  transfers between devices with their start and end apart: 15, of which 10 were waited for; matrix products, arithmetic and copies ran while one was open for 30% of the time, Pallas kernels for 0%

commit v1 on v0

v1 whole, which is shorter than its diff:
```python
import functools

import jax
import jax.numpy as jnp
from jax import lax
from jax.experimental import pallas as pl
from jax.experimental.pallas import tpu as pltpu
from jax.sharding import PartitionSpec as P

HEAD_DIM = 64
SPAN = 8
PAIR = 2 * HEAD_DIM
THETA = 160000.0
EPS = 1e-05
SCALE = 0.125
MASKED = -1e30
BLOCK = 256
BOTH = ("shard", "rep")


def norm_rows(values, gain_vec):
    centered = values - jnp.mean(values, axis=-1, keepdims=True)
    variance = jnp.mean(centered * centered, axis=-1, keepdims=True)
    return centered * lax.rsqrt(variance + EPS) * gain_vec


def gated_units(pre_act):
    units = pre_act.shape[1] // 2
    return jax.nn.gelu(pre_act[:, :units], approximate=False) * pre_act[:, units:]


def gather_weight(shard):
    copies = lax.axis_size("rep")
    mine = lax.axis_index("rep")
    rows, cols = shard.shape
    if rows % (8 * copies) == 0:
        part = lax.dynamic_slice_in_dim(shard, mine * (rows // copies), rows // copies)
        return lax.all_gather(part, BOTH, axis=0, tiled=True)
    flat = shard.reshape(rows * cols // 128, 128)
    count = flat.shape[0] // copies
    part = lax.dynamic_slice_in_dim(flat, mine * count, count)
    return lax.all_gather(part, BOTH, axis=0, tiled=True).reshape(-1, cols)


def scatter_grad(grad, rows):
    copies = lax.axis_size("rep")
    if rows % (8 * copies) == 0:
        return lax.psum_scatter(grad, BOTH, scatter_dimension=0, tiled=True)
    flat = grad.reshape(-1, 128)
    return lax.psum_scatter(flat, BOTH, scatter_dimension=0, tiled=True)


def finish_grad(share, rows):
    whole = lax.all_gather(share, "rep", axis=0, tiled=True)
    return whole.reshape(rows, -1).astype(jnp.float32)


def exchange(blocks):
    size = lax.axis_size("shard")
    groups = [list(range(first, first + SPAN)) for first in range(0, size, SPAN)]
    return lax.all_to_all(
        blocks, "shard", 0, 0, tiled=False, axis_index_groups=groups if size > SPAN else None
    )


def lanes(shape):
    return lax.broadcasted_iota(jnp.int32, shape, len(shape) - 1)


def turned(values, cosine, sine):
    lower = lanes(values.shape) % HEAD_DIM < HEAD_DIM // 2
    other = jnp.where(
        lower,
        pltpu.roll(values, PAIR - HEAD_DIM // 2, 1),
        pltpu.roll(values, HEAD_DIM // 2, 1),
    )
    return values * cosine + other * sine


def project_body(n_ref, wq_ref, wk_ref, wv_ref, cos_ref, sin_ref, out_ref):
    rows = n_ref[...]
    for part, w_ref in enumerate((wq_ref, wk_ref, wv_ref)):
        result = jnp.dot(rows, w_ref[...], preferred_element_type=jnp.float32)
        for pair in range(result.shape[1] // PAIR):
            piece = result[:, pair * PAIR : (pair + 1) * PAIR]
            if part < 2:
                piece = turned(piece, cos_ref[...], sin_ref[...])
            out_ref[pair, :, part * PAIR : (part + 1) * PAIR] = piece.astype(jnp.bfloat16)


def project(normed, weight, cosine, sine):
    rows, width = normed.shape
    step = 2
    steps = SPAN // step
    w_spec = lambda part: pl.BlockSpec(
        (width, step * PAIR), lambda d: (0, part * steps + d)
    )
    whole = lambda array: pl.BlockSpec(array.shape, lambda d: (0, 0))
    return pl.pallas_call(
        project_body,
        grid=(steps,),
        in_specs=[whole(normed), w_spec(0), w_spec(1), w_spec(2), whole(cosine), whole(sine)],
        out_specs=pl.BlockSpec((step, rows, 3 * PAIR), lambda d: (d, 0, 0)),
        out_shape=jax.ShapeDtypeStruct((SPAN, rows, 3 * PAIR), jnp.bfloat16),
        name="project_heads",
    )(normed, weight, weight, weight, cosine, sine)


def nt_dot(a, b):
    return lax.dot_general(a, b, (((1,), (1,)), ((), ())), preferred_element_type=jnp.float32)


def tn_dot(a, b):
    return lax.dot_general(a, b, (((0,), (0,)), ((), ())), preferred_element_type=jnp.float32)


def attend_body(lo_ref, hi_ref, qkv_ref, segc_ref, segr_ref, out_ref, lse_ref, acc_ref, max_ref):
    block = BLOCK
    first_head = lanes((block, PAIR)) < HEAD_DIM

    def query_step(i, _):
        at = pl.ds(pl.multiple_of(i * block, block), block)
        query = qkv_ref[at, :PAIR] * jnp.bfloat16(SCALE)
        zero = jnp.zeros_like(query)
        queries = (jnp.where(first_head, query, zero), jnp.where(first_head, zero, query))
        own = jnp.concatenate([segc_ref[at, :]] * (block // 128), axis=1)
        for head in range(2):
            acc_ref[head] = jnp.zeros((block, PAIR), jnp.float32)
            max_ref[head] = jnp.full((block, 128), MASKED, jnp.float32)

        def key_step(j, _):
            there = pl.ds(pl.multiple_of(j * block, block), block)
            key = qkv_ref[there, PAIR : 2 * PAIR]
            value = qkv_ref[there, 2 * PAIR :]
            one = jnp.ones_like(value)
            values = (jnp.where(first_head, value, one), jnp.where(first_head, one, value))
            same = own == segr_ref[0:1, there]
            for head in range(2):
                scores = jnp.where(same, nt_dot(queries[head], key), MASKED)
                before = max_ref[head]
                now = jnp.maximum(before, jnp.max(scores, axis=1, keepdims=True))
                wide = jnp.concatenate([now] * (block // 128), axis=1)
                weights = jnp.exp(scores - wide).astype(jnp.bfloat16)
                gained = jnp.dot(weights, values[head], preferred_element_type=jnp.float32)
                acc_ref[head] = acc_ref[head] * jnp.exp(before - now) + gained
                max_ref[head] = now
            return 0

        lax.fori_loop(lo_ref[i], hi_ref[i], key_step, 0)
        first, second = acc_ref[0], acc_ref[1]
        top = jnp.where(first_head, first, second)
        total = jnp.where(first_head, pltpu.roll(first, HEAD_DIM, 1), pltpu.roll(second, HEAD_DIM, 1))
        out_ref[at, :] = (top / total).astype(jnp.bfloat16)
        lse = jnp.where(first_head, max_ref[0], max_ref[1]) + jnp.log(total)
        flipped = lse.T
        lse_ref[0:1, at] = flipped[0:1]
        lse_ref[1:2, at] = flipped[HEAD_DIM : HEAD_DIM + 1]
        return 0

    lax.fori_loop(0, out_ref.shape[0] // block, query_step, 0)


def spec_smem():
    return pl.BlockSpec(memory_space=pltpu.SMEM)


def spec_vmem():
    return pl.BlockSpec(memory_space=pltpu.VMEM)


def attend(qkv, lows, highs, seg_col, seg_row):
    length = qkv.shape[0]
    return pl.pallas_call(
        attend_body,
        in_specs=[spec_smem(), spec_smem()] + [spec_vmem()] * 3,
        out_specs=[spec_vmem()] * 2,
        out_shape=[
            jax.ShapeDtypeStruct((length, PAIR), jnp.bfloat16),
            jax.ShapeDtypeStruct((8, length), jnp.float32),
        ],
        scratch_shapes=[
            pltpu.VMEM((2, BLOCK, PAIR), jnp.float32),
            pltpu.VMEM((2, BLOCK, 128), jnp.float32),
        ],
        name="attend_forward",
    )(lows, highs, qkv, seg_col, seg_row)


def attend_back_body(
    lo_ref, hi_ref, qkv_ref, out_ref, grad_ref, lse_ref, segc_ref, segr_ref, cos_ref, sin_ref,
    res_ref, dq_ref, dk_ref, dv_ref, sum_ref,
):
    block = BLOCK
    length = qkv_ref.shape[0]
    first_head = lanes((block, PAIR)) < HEAD_DIM
    sub = lax.broadcasted_iota(jnp.int32, (8, PAIR), 0)
    picks = (lanes((8, PAIR)) // HEAD_DIM == sub).astype(jnp.float32)

    def prepare(i, _):
        at = pl.ds(pl.multiple_of(i * block, block), block)
        product = grad_ref[at, :].astype(jnp.float32) * out_ref[at, :].astype(jnp.float32)
        sum_ref[:, at] = lax.dot_general(
            picks, product, (((1,), (1,)), ((), ())),
            precision=lax.Precision.HIGHEST, preferred_element_type=jnp.float32,
        )
        dq_ref[at, :] = jnp.zeros((block, PAIR), jnp.float32)
        return 0

    lax.fori_loop(0, length // block, prepare, 0)

    def key_step(j, _):
        at = pl.ds(pl.multiple_of(j * block, block), block)
        key = qkv_ref[at, PAIR : 2 * PAIR]
        value = qkv_ref[at, 2 * PAIR :]
        zero = jnp.zeros_like(key)
        keys = (jnp.where(first_head, key, zero), jnp.where(first_head, zero, key))
        own = jnp.concatenate([segc_ref[at, :]] * (block // 128), axis=1)
        dk_ref[...] = jnp.zeros((block, PAIR), jnp.float32)
        dv_ref[...] = jnp.zeros((block, PAIR), jnp.float32)

        def query_step(i, _):
            there = pl.ds(pl.multiple_of(i * block, block), block)
            query = qkv_ref[there, :PAIR] * jnp.bfloat16(SCALE)
            grad = grad_ref[there, :]
            queries = (jnp.where(first_head, query, zero), jnp.where(first_head, zero, query))
            grads = (jnp.where(first_head, grad, zero), jnp.where(first_head, zero, grad))
            same = own == segr_ref[0:1, there]
            dv, dk, dq = dv_ref[...], dk_ref[...], dq_ref[there, :]
            for head in range(2):
                scores = jnp.where(same, nt_dot(key, queries[head]), MASKED)
                weights = jnp.exp(scores - lse_ref[head : head + 1, there])
                pulled = nt_dot(value, grads[head])
                slopes = (weights * (pulled - sum_ref[head : head + 1, there])).astype(jnp.bfloat16)
                dv = dv + jnp.dot(weights.astype(jnp.bfloat16), grads[head], preferred_element_type=jnp.float32)
                dk = dk + jnp.dot(slopes, queries[head], preferred_element_type=jnp.float32)
                dq = dq + tn_dot(slopes, keys[head])
            dv_ref[...] = dv
            dk_ref[...] = dk
            dq_ref[there, :] = dq
            return 0

        lax.fori_loop(lo_ref[j], hi_ref[j], query_step, 0)
        res_ref[at, PAIR : 2 * PAIR] = turned(dk_ref[...], cos_ref[at, :], -sin_ref[at, :]).astype(jnp.bfloat16)
        res_ref[at, 2 * PAIR :] = dv_ref[...].astype(jnp.bfloat16)
        return 0

    lax.fori_loop(0, length // block, key_step, 0)

    def finish(i, _):
        at = pl.ds(pl.multiple_of(i * block, block), block)
        res_ref[at, :PAIR] = turned(dq_ref[at, :] * SCALE, cos_ref[at, :], -sin_ref[at, :]).astype(jnp.bfloat16)
        return 0

    lax.fori_loop(0, length // block, finish, 0)


def attend_back(qkv, out, grad, lse, lows, highs, seg_col, seg_row, cosine, sine):
    length = qkv.shape[0]
    return pl.pallas_call(
        attend_back_body,
        in_specs=[spec_smem(), spec_smem()] + [spec_vmem()] * 8,
        out_specs=spec_vmem(),
        out_shape=jax.ShapeDtypeStruct((length, 3 * PAIR), jnp.bfloat16),
        scratch_shapes=[
            pltpu.VMEM((length, PAIR), jnp.float32),
            pltpu.VMEM((BLOCK, PAIR), jnp.float32),
            pltpu.VMEM((BLOCK, PAIR), jnp.float32),
            pltpu.VMEM((8, length), jnp.float32),
        ],
        name="attend_backward",
    )(lows, highs, qkv, out, grad, lse, seg_col, seg_row, cosine, sine)


def local(tokens, seg_ids, w_qkv, w_out, w_in, w_down, attn_gain, ffn_gain, cotangent):
    f32, bf16 = jnp.float32, jnp.bfloat16
    rows, width = tokens.shape
    length = SPAN * rows
    position = lax.axis_index("shard")
    offset = position % SPAN

    full_qkv = gather_weight(w_qkv)
    placed = jnp.zeros((2, width), f32)
    placed = lax.dynamic_update_slice(
        placed, jnp.stack([attn_gain, ffn_gain]).astype(f32), (0, position * attn_gain.shape[0])
    )
    gains = lax.psum(placed, "shard")
    gain_one, gain_two = gains[0], gains[1]
    full_out = gather_weight(w_out)
    full_in = gather_weight(w_in)
    full_down = gather_weight(w_down)

    lane = jnp.arange(PAIR, dtype=jnp.int32)
    half = HEAD_DIM // 2
    frequency = THETA ** (-((lane % half).astype(f32) * 2.0 / HEAD_DIM))
    angles = jnp.arange(length, dtype=jnp.int32).astype(f32)[:, None] * frequency[None, :]
    cosine = jnp.cos(angles)
    sine = jnp.sin(angles) * jnp.where(lane % HEAD_DIM < half, -1.0, 1.0)
    here = offset * rows
    cosine_here = lax.dynamic_slice_in_dim(cosine, here, rows)
    sine_here = lax.dynamic_slice_in_dim(sine, here, rows)
    segments = lax.dynamic_slice_in_dim(seg_ids, (position - offset) * rows, length)
    seg_col = jnp.broadcast_to(segments[:, None], (length, 128))
    seg_row = jnp.broadcast_to(segments[None, :], (8, length))
    firsts, lasts = segments[::BLOCK], segments[BLOCK - 1 :: BLOCK]
    lows = jnp.sum(segments[None, :] < firsts[:, None], axis=1, dtype=jnp.int32) // BLOCK
    highs = (jnp.sum(segments[None, :] <= lasts[:, None], axis=1, dtype=jnp.int32) + BLOCK - 1) // BLOCK

    resid_in = tokens.astype(f32)
    normed_one = norm_rows(resid_in, gain_one).astype(bf16)
    sent = project(normed_one, full_qkv, cosine_here, sine_here)
    qkv = exchange(sent).reshape(length, 3 * PAIR)
    out_heads, lse = attend(qkv, lows, highs, seg_col, seg_row)
    attn_low = jnp.transpose(
        exchange(out_heads.reshape(SPAN, rows, PAIR)), (1, 0, 2)
    ).reshape(rows, width)
    resid_mid = resid_in + jnp.dot(attn_low, full_out, preferred_element_type=f32)

    normed_two = norm_rows(resid_mid, gain_two).astype(bf16)
    pre_act = jnp.dot(normed_two, full_in, preferred_element_type=f32)
    units_low = gated_units(pre_act).astype(bf16)
    layer_out = (resid_mid + jnp.dot(units_low, full_down, preferred_element_type=f32)).astype(bf16)

    grad_units_low = jnp.einsum("td,fd->tf", cotangent, full_down, preferred_element_type=f32).astype(bf16)
    pull_gate = jax.vjp(gated_units, pre_act)[1]
    grad_pre = pull_gate(grad_units_low.astype(f32))[0].astype(bf16)
    grad_normed_two = jnp.einsum("tf,df->td", grad_pre, full_in, preferred_element_type=f32).astype(bf16)
    pull_norm_two = jax.vjp(norm_rows, resid_mid, gain_two)[1]
    grad_mid_norm, grad_gain_two = pull_norm_two(grad_normed_two.astype(f32))
    grad_resid = cotangent.astype(f32) + grad_mid_norm
    grad_branch_low = grad_resid.astype(bf16)
    grad_attn = jnp.einsum("te,de->td", grad_branch_low, full_out, preferred_element_type=f32).astype(bf16)
    grad_heads = exchange(jnp.transpose(grad_attn.reshape(rows, SPAN, PAIR), (1, 0, 2)))
    grad_heads = grad_heads.reshape(length, PAIR)

    grad_down = jnp.einsum("tf,td->fd", units_low, cotangent, preferred_element_type=f32).astype(bf16)
    grad_in = jnp.einsum("td,tf->df", normed_two, grad_pre, preferred_element_type=f32).astype(bf16)
    grad_out = jnp.einsum("td,te->de", attn_low, grad_branch_low, preferred_element_type=f32).astype(bf16)
    share_down = scatter_grad(grad_down, w_down.shape[0])
    share_in = scatter_grad(grad_in, w_in.shape[0])
    share_out = scatter_grad(grad_out, w_out.shape[0])

    slopes = attend_back(qkv, out_heads, grad_heads, lse, lows, highs, seg_col, seg_row, cosine, sine)
    back = exchange(slopes.reshape(SPAN, rows, 3 * PAIR))
    grad_proj = jnp.transpose(back.reshape(SPAN, rows, 3, PAIR), (1, 2, 0, 3)).reshape(rows, 3 * width)
    grad_qkv = jnp.einsum("td,tf->df", normed_one, grad_proj, preferred_element_type=f32).astype(bf16)
    share_qkv = scatter_grad(grad_qkv, w_qkv.shape[0])
    grad_normed_one = jnp.einsum("tf,df->td", grad_proj, full_qkv, preferred_element_type=f32).astype(bf16)
    pull_norm_one = jax.vjp(norm_rows, resid_in, gain_one)[1]
    grad_in_norm, grad_gain_one = pull_norm_one(grad_normed_one.astype(f32))
    grad_tokens = (grad_resid + grad_in_norm).astype(bf16)

    gain_sums = lax.psum(jnp.stack([grad_gain_one, grad_gain_two]), BOTH)
    gain_rows = attn_gain.shape[0]
    gain_sums = lax.dynamic_slice_in_dim(gain_sums, position * gain_rows, gain_rows, axis=1)
    return (
        layer_out,
        grad_tokens,
        gain_sums[0],
        gain_sums[1],
        finish_grad(share_qkv, w_qkv.shape[0]),
        finish_grad(share_out, w_out.shape[0]),
        finish_grad(share_in, w_in.shape[0]),
        finish_grad(share_down, w_down.shape[0]),
    )


def solution(mesh):
    row = P(("rep", "shard"), None)
    weight = P("shard", None)
    in_specs = (row, P("rep"), weight, weight, weight, weight, P("shard"), P("shard"), row)
    out_specs = (row, row, P("shard"), P("shard"), weight, weight, weight, weight)
    return jax.shard_map(local, mesh=mesh, in_specs=in_specs, out_specs=out_specs, check_vma=False)
```

time: 2810 us -> 1030 us (0.37)
  waiting for transfers between devices: 1610 us -> 416 us
  matrix products: 569 us -> 97.4 us
  other arithmetic: 250 us -> 28.7 us
  Pallas kernels: 0 us -> 179 us
  local copies, waits for them, and re-layouts: 86.5 us -> 47.6 us
  blocking collectives: 254 us -> 219 us
    ppermute x6 -> x0, waiting for transfers between devices: 978 us -> none  [swapped(): lax.ppermute(shard, axis, [(i, i ^ 1 << stride) for i in range(lax.axis_s...]
    dot_general x123 -> x10, matrix products: 566 us -> 94.8 us  [the longest x1 17.1 us: local(): jnp.einsum('td,fd->tf', cotangent, full_down, preferred_element_type=f32)]
    reduce_scatter x4, waiting for transfers between devices: 529 us -> 222 us  [the longest x3 121 us: scatter_grad(): return lax.psum_scatter(grad, BOTH, scatter_dimension=0, tiled=True)]
    all_gather x2 -> x3, blocking collectives: 229 us -> 43.2 us  [finish_grad(): whole = lax.all_gather(share, 'rep', axis=0, tiled=True)]
    pallas_call x0 -> x3, Pallas kernels: none -> 179 us  [the longest x1 93.6 us: attend_back(): pl.pallas_call(attend_back_body, in_specs=[spec_smem(), spec_smem()] + [s...]
    convert_element_type x34 -> x7, other arithmetic: 163 us -> 10.2 us  [the longest x3 5.15 us: finish_grad(): return whole.reshape(rows, -1).astype(jnp.float32)]
    all_to_all x0 -> x2, blocking collectives: none -> 107 us  [exchange(): lax.all_to_all(blocks, 'shard', 0, 0, tiled=False, axis_index_groups=grou...]
    all_to_all x0 -> x2, waiting for transfers between devices: none -> 98.8 us  [exchange(): lax.all_to_all(blocks, 'shard', 0, 0, tiled=False, axis_index_groups=grou...]
  transfers between devices with their start and end apart: 15 -> 11, of which waited for: 10 -> 8; matrix products, arithmetic and copies ran while one was open for 30% -> 10% of each run, Pallas kernels for 0% -> 18%
where the time goes in v1:
time: 1030 us; the launch traced here: 1010 us
  waiting for transfers between devices  416 us (40%)
  blocking collectives  219 us (21%)
  Pallas kernels  179 us (17%)
  matrix products  97.4 us (9%)
  local copies, waits for them, and re-layouts  47.6 us (5%)
  other arithmetic  28.7 us (3%)
  between operations  14.6 us (1%)
    reduce_scatter x3, waiting for transfers between devices, scatter_grad(): return lax.psum_scatter(grad, BOTH, scatter_dimension=0, tiled=True)  121 us
    all_to_all x2, blocking collectives, exchange(): lax.all_to_all(blocks, 'shard', 0, 0, tiled=False, axis_index_groups=grou...  107 us
    reduce_scatter x1, waiting for transfers between devices, scatter_grad(): return lax.psum_scatter(flat, BOTH, scatter_dimension=0, tiled=True)  100 us
    all_to_all x2, waiting for transfers between devices, exchange(): lax.all_to_all(blocks, 'shard', 0, 0, tiled=False, axis_index_groups=grou...  98.8 us
    pallas_call x1, Pallas kernels, attend_back(): pl.pallas_call(attend_back_body, in_specs=[spec_smem(), spec_smem()] + [s...  93.6 us
    all_gather x3, waiting for transfers between devices, gather_weight(): return lax.all_gather(part, BOTH, axis=0, tiled=True)  86.9 us
    pallas_call x1, Pallas kernels, attend(): pl.pallas_call(attend_body, in_specs=[spec_smem(), spec_smem()] + [spec_v...  77.5 us
    psum x1, blocking collectives, local(): gain_sums = lax.psum(jnp.stack([grad_gain_one, grad_gain_two]), BOTH)  46.3 us
  transfers between devices with their start and end apart: 11, of which 8 were waited for; matrix products, arithmetic and copies ran while one was open for 10% of the time, Pallas kernels for 18%

profile of v1, /device:TPU:0, one launch (start us, length us, event | category | flops | bytes accessed | tf_op | source)
XLA Modules:
  0.0 1012.3 jit_solution(3133565505892616120)
XLA Ops:
  7.2 1.8 constant_dynamic-slice_fusion.6
  9.1 1.4 reshape.145
  10.5 0.7 constant_dynamic-slice_fusion.1
  11.2 1.5 constant_dynamic-slice_fusion.3
  12.8 0.8 constant_dynamic-slice_fusion.2
  13.6 0.7 constant_dynamic-update-slice_fusion
  14.3 23.4 %psum.14 = f32[2,1024]{1,0:T(2,128)S(1)} all-reduce(f32[2,1024]{1,0:T(2,128)S(1)} %constant_dynamic-update-slice_fusion), channel_id=1, replica_groups=mesh['rep'=4,'shard'=8] {'shard'}, use_global_device_ids=true, to_apply=%region_4.5 | all-reduce | flops 2048 | bytes 16384 | tf_op jit(solution)/shard_map/psum | solution.py:286
  37.8 7.4 fusion.19
  45.2 1.3 copy-done.6
  46.5 0.7 constant_dynamic-slice_fusion.4.sin_ref
  47.3 0.7 constant_dynamic-slice_fusion.5.cos_ref
  48.6 0.6 copy-done.20
  49.2 1.3 fusion.15.n_ref
  50.6 33.1 %all-gather.6.cloned.1.call-done.wq_ref.wk_ref.wv_ref = bf16[1024,3072]{1,0:T(8,128)(2,1)} async-done(((bf16[32,3072]{1,0:T(8,128)(2,1)}), bf16[1024,3072]{1,0:T(8,128)(2,1)}) %all-gather.6.cloned.1.call-update) | async-done | bytes 6291472 | tf_op jit(solution)/shard_map/all_gather | solution.py:38
  83.7 8.4 project_heads.1
  92.0 4.6 all-to-all-start
  97.1 0.5 and_select_fusion.2
  97.6 91.8 %all-to-all-done = bf16[8,512,384]{2,1,0:T(8,128)(2,1)} async-done(((bf16[8,512,384]{2,1,0:T(8,128)(2,1)}), bf16[8,512,384]{2,1,0:T(8,128)(2,1)}, u32[]{:S(2)}, u32[]{:S(2)}) %all-to-all-start) | async-done | bytes 3145760 | tf_op jit(solution)/shard_map/all_to_all | solution.py:61
  189.4 0.7 broadcast_in_dim.26.segr_ref
  190.1 2.9 broadcast_in_dim.25.segc_ref
  193.1 77.5 %attend_forward.1 = (bf16[4096,128]{1,0:T(8,128)(2,1)}, f32[8,4096]{1,0:T(8,128)}) custom-call(s32[16]{0:T(128)} %get-tuple-element.37.lo_ref, s32[16]{0:T(128)} %get-tuple-element.36.hi_ref, bf16[4096,384]{1,0:T(8,128)(2,1)} %bitcast.3.qkv_ref, s32[4096,128]{1,0:T(8,128)} %broadcast_in_dim.25.segc_ref, s32[8,4096]{1,0:T(8,128)} %broadcast_in_dim.26.segr_ref), custom_call_target="tpu_custom_call" | custom-call | tf_op jit(solution)/shard_map/attend_forward/pallas_call | solution.py:173
  270.5 2.3 copy.29
  272.8 3.6 all-to-all-start.1
  276.9 9.2 reshape.146
  286.1 6.9 all-to-all-done.1
  293.1 2.9 fusion.37
  296.0 1.3 copy-done.3
  297.7 53.8 %all-gather.10.cloned.1.call-done = bf16[1024,5248]{1,0:T(8,128)(2,1)} async-done(((bf16[32,5248]{1,0:T(8,128)(2,1)}), bf16[1024,5248]{1,0:T(8,128)(2,1)}) %all-gather.10.cloned.1.call-update) | async-done | bytes 10747920 | tf_op jit(solution)/shard_map/all_gather | solution.py:38
  351.6 15.8 %fusion.33 = f32[512,5248]{0,1:T(8,128)} fusion(bf16[1024,5248]{1,0:T(8,128)(2,1)} %all-gather.10.cloned.1.call-done, f32[512,1024]{1,0:T(8,128)} %copy-done.3, f32[1024]{0:T(1024)S(1)} %bitcast.66, f32[512]{0:T(512)S(1)} %fusion.26, f32[512]{0:T(512)S(1)} %broadcast_multiply_fusion), kind=kOutput, calls=%fused_computation.106 | convolution fusion | flops 5505024000 | bytes 23601152 | tf_op jit(solution)/shard_map/dot_general | solution.py:319
  367.3 17.1 %bitcast_multiply_fusion.1 = (f32[512,2624]{0,1:T(8,128)}, f32[512,2624]{0,1:T(8,128)S(1)}, bf16[2624,512]{1,0:T(8,128)(2,1)S(1)}) fusion(f32[512,5248]{0,1:T(8,128)} %fusion.33, bf16[2624,1024]{1,0:T(8,128)(2,1)} %reshape.146, bf16[512,1024]{1,0:T(8,128)(2,1)S(1)} %copy-done.9), kind=kOutput, calls=%fused_computation.7 | convolution fusion | flops 2841477120 | bytes 25231360 | tf_op jit(solution)/shard_map/td,fd->tf/dot_general | solution.py:323
  384.5 4.9 multiply_add_fusion
  389.3 13.4 %fusion.17 = (f32[1024]{0:T(1024)S(1)}, f32[512]{0:T(512)S(1)}, bf16[512,1024]{1,0:T(8,128)(2,1)}) fusion(f32[512,1024]{1,0:T(8,128)} %copy-done.3, f32[512]{0:T(512)S(1)} %fusion.26, f32[512]{0:T(512)S(1)} %broadcast_multiply_fusion, f32[1024]{0:T(1024)S(1)} %bitcast.67, bf16[1024,5248]{1,0:T(8,128)(2,1)} %all-gather.10.cloned.1.call-done, ...), kind=kOutput, calls=%fused_computation.47 | convolution fusion | flops 5513017856 | bytes 24655872 | tf_op jit(solution)/shard_map/tf,df->td/dot_general | solution.py:326
  402.8 2.6 fusion.34
  405.4 1.3 copy-done.4
  407.1 1.0 copy-done.11
  408.0 2.6 convolution_convert_fusion.4
  410.7 14.8 %convolution_convert_fusion = bf16[1024,5248]{1,0:T(8,128)(2,1)} fusion(f32[512,2624]{0,1:T(8,128)} %get-tuple-element.22, f32[512,2624]{0,1:T(8,128)} %get-tuple-element.20, f32[512,1024]{1,0:T(8,128)} %copy-done.3, f32[1024]{0:T(1024)S(1)} %bitcast.69, f32[512]{0:T(512)S(1)} %fusion.26, f32[512]{0:T(512)S(1)} %broadcast_multiply_fusion), kind=kOutput, calls=%fused_computation | convolution fusion | flops 5515771904 | bytes 23601152 | tf_op jit(solution)/shard_map/td,tf->df/dot_general | solution.py:336
  425.5 6.7 convolution_convert_fusion.1
  432.2 9.2 reshape.154
  441.5 1.2 copy-done.12
  442.7 2.9 fusion.22
  445.7 32.3 %all_to_all.20 = bf16[8,512,128]{2,1,0:T(8,128)(2,1)} all-to-all(bf16[8,512,128]{2,1,0:T(8,128)(2,1)S(1)} %bitcast.56), channel_id=1, replica_groups=mesh['rep'=4,'shard'=8] {'shard'}, dimensions={0} | all-to-all | bytes 2097152 | tf_op jit(solution)/shard_map/all_to_all | solution.py:61
  478.1 93.6 %attend_backward.1 = bf16[4096,384]{1,0:T(8,128)(2,1)} custom-call(s32[16]{0:T(128)} %get-tuple-element.37.lo_ref, s32[16]{0:T(128)} %get-tuple-element.36.hi_ref, bf16[4096,384]{1,0:T(8,128)(2,1)} %bitcast.3.qkv_ref, bf16[4096,128]{1,0:T(8,128)(2,1)} %get-tuple-element.10.out_ref, bf16[4096,128]{1,0:T(8,128)(2,1)} %bitcast.55, ...), custom_call_target="tpu_custom_call" | custom-call | tf_op jit(solution)/shard_map/attend_backward/pallas_call | solution.py:259
  571.6 4.7 copy.33
  576.3 74.3 %all_to_all.21 = bf16[8,512,384]{1,2,0:T(8,128)(2,1)S(1)} all-to-all(bf16[8,512,384]{1,2,0:T(8,128)(2,1)} %copy.33), channel_id=1, replica_groups=mesh['rep'=4,'shard'=8] {'shard'}, dimensions={0} | all-to-all | bytes 6291456 | tf_op jit(solution)/shard_map/all_to_all | solution.py:61
  650.9 1.7 copy-done.10
  652.6 5.4 convolution_convert_fusion.2
  658.1 8.2 add_convert_fusion.2
  666.3 27.2 %all_gather.29 = bf16[128,1024]{1,0:T(8,128)(2,1)S(1)} all-gather(bf16[32,1024]{1,0:T(8,128)(2,1)} %reduce-scatter.7.cloned.1.call-done), channel_id=1, replica_groups=mesh['rep'=4,'shard'=8] {'rep'}, dimensions={0}, use_global_device_ids=true | all-gather | bytes 327680 | tf_op jit(solution)/shard_map/all_gather | solution.py:54
  693.5 0.8 convert_element_type.139
  694.4 7.6 fusion.21
  702.0 13.0 %reduce-scatter.9.cloned.1.call-done = bf16[32,5248]{1,0:T(8,128)(2,1)} async-done(((bf16[1024,5248]{1,0:T(8,128)(2,1)}), bf16[32,5248]{1,0:T(8,128)(2,1)}) %reduce-scatter.9.cloned.1.call-update) | async-done | bytes 335888 | tf_op jit(solution)/shard_map/reduce_scatter | solution.py:48
  715.0 1.2 fusion.18
  716.3 46.3 %psum.15 = f32[2,1024]{1,0:T(2,128)S(1)} all-reduce(f32[2,1024]{1,0:T(2,128)S(1)} %pad_maximum_fusion), channel_id=1, replica_groups=mesh['rep'=4,'shard'=8] {'shard','rep'}, use_global_device_ids=true, to_apply=%region_13.14 | all-reduce | flops 2048 | bytes 16384 | tf_op jit(solution)/shard_map/psum | solution.py:352
  762.6 0.5 slice_bitcast_fusion
  763.1 3.4 add_convert_fusion.1
  766.5 100.3 %reduce-scatter.11.cloned.1.call-done = bf16[656,128]{1,0:T(8,128)(2,1)} async-done(((bf16[20992,128]{1,0:T(8,128)(2,1)}), bf16[656,128]{1,0:T(8,128)(2,1)}) %reduce-scatter.11.cloned.1.call-update) | async-done | bytes 167952 | tf_op jit(solution)/shard_map/reduce_scatter | solution.py:50
  866.8 7.1 all_gather.31
  873.9 1.3 reshape.155
  875.3 108.2 %reduce-scatter.5.cloned.1.call-done = bf16[32,3072]{1,0:T(8,128)(2,1)} async-done(((bf16[1024,3072]{1,0:T(8,128)(2,1)}), bf16[32,3072]{1,0:T(8,128)(2,1)}) %reduce-scatter.5.cloned.1.call-update) | async-done | bytes 196624 | tf_op jit(solution)/shard_map/reduce_scatter | solution.py:48
  983.4 8.8 all_gather.28
  992.3 1.3 convert_element_type.137
  993.6 8.8 all-gather.14.cloned.1.call-done
  1002.3 3.0 convert_element_type.141
  (81 shorter events, 3.4 us)
Async XLA Ops:
  7.2 5.6 copy-start
  7.2 40.8 %copy-start.2 = (bf16[512,1024]{1,0:T(8,128)(2,1)S(1)}, bf16[512,1024]{1,0:T(8,128)(2,1)}, u32[]{:S(2)}) copy-start(bf16[512,1024]{1,0:T(8,128)(2,1)} %param.9) | copy-start | bytes 3145732
  7.2 76.5 %all-gather.6.cloned.1.call-start = ((), (), s32[]{:S(2)}) async-start(), calls=%async_computation.8 | async-start | bytes 6488064 | tf_op jit(solution)/shard_map/all_gather | solution.py:38
  9.0 267.8 %all-gather.12.cloned.1.call-start = ((), (), s32[]{:S(2)}) async-start(), calls=%async_computation.11 | async-start | bytes 5541888 | tf_op jit(solution)/shard_map/all_gather | solution.py:42
  11.2 274.9 %all-gather.8.cloned.1.call-start = ((), (), s32[]{:S(2)}) async-start(), calls=%async_computation.9 | async-start | bytes 2162688 | tf_op jit(solution)/shard_map/all_gather | solution.py:38
  12.8 338.8 %all-gather.10.cloned.1.call-start = ((), (), s32[]{:S(2)}) async-start(), calls=%async_computation.10 | async-start | bytes 11083776 | tf_op jit(solution)/shard_map/all_gather | solution.py:38
  45.2 1.3 copy-start.6
  45.2 2.1 copy-start.7
  48.2 35.5 %copy-start.16 = (f32[512]{0:T(512)}, f32[512]{0:T(512)S(1)}, u32[]{:S(2)}) copy-start(f32[512]{0:T(512)S(1)} %broadcast_multiply_fusion.1) | copy-start | bytes 6148
  48.6 0.6 copy-start.20
  49.2 34.5 %copy-start.18 = (f32[512]{0:T(512)}, f32[512]{0:T(512)S(1)}, u32[]{:S(2)}) copy-start(f32[512]{0:T(512)S(1)} %fusion.25) | copy-start | bytes 6148
  49.2 34.4 %copy-start.14 = (f32[1,1024]{1,0:T(1,128)}, f32[1,1024]{1,0:T(1,128)S(1)}, u32[]{:S(2)}) copy-start(f32[1,1024]{1,0:T(1,128)S(1)} %get-tuple-element.27) | copy-start | bytes 12292
  92.0 4.6 copy-start.13
  92.0 97.4 %all-to-all-start = ((bf16[8,512,384]{2,1,0:T(8,128)(2,1)}), bf16[8,512,384]{2,1,0:T(8,128)(2,1)}, u32[]{:S(2)}, u32[]{:S(2)}) async-start(bf16[8,512,384]{2,1,0:T(8,128)(2,1)} %project_heads.1), calls=%async_computation | async-start | bytes 6291456 | tf_op jit(solution)/shard_map/all_to_all | solution.py:61
  272.8 20.3 %all-to-all-start.1 = ((bf16[8,512,128]{1,2,0:T(8,128)(2,1)}), bf16[8,512,128]{1,2,0:T(8,128)(2,1)S(1)}, u32[]{:S(2)}, u32[]{:S(2)}) async-start(bf16[8,512,128]{1,2,0:T(8,128)(2,1)} %copy.29), calls=%async_computation.1 | async-start | bytes 2097152 | tf_op jit(solution)/shard_map/all_to_all | solution.py:61
  276.4 389.9 %reduce-scatter.7.cloned.1.call-start = ((), (), s32[]{:S(2)}) async-start(), calls=%async_computation.13 | async-start | bytes 2162688 | tf_op jit(solution)/shard_map/reduce_scatter | solution.py:48
  296.0 1.4 copy-start.3
  351.6 15.8 %copy-start.9 = (bf16[512,1024]{1,0:T(8,128)(2,1)S(1)}, bf16[512,1024]{1,0:T(8,128)(2,1)}, u32[]{:S(2)}) copy-start(bf16[512,1024]{1,0:T(8,128)(2,1)} %param.17) | copy-start | bytes 3145732
  367.3 17.1 %copy-start.5 = (f32[512,5248]{0,1:T(8,128)S(1)}, f32[512,5248]{0,1:T(8,128)}, u32[]{:S(2)}) copy-start(f32[512,5248]{0,1:T(8,128)} %fusion.33) | copy-start | bytes 32243716
  405.4 1.4 copy-start.4
  407.1 1.0 copy-start.11
  410.6 304.4 %reduce-scatter.9.cloned.1.call-start = ((), (), s32[]{:S(2)}) async-start(), calls=%async_computation.14 | async-start | bytes 11083776 | tf_op jit(solution)/shard_map/reduce_scatter | solution.py:48
  425.5 441.3 %reduce-scatter.11.cloned.1.call-start = ((), (), s32[]{:S(2)}) async-start(), calls=%async_computation.16 | async-start | bytes 5541888 | tf_op jit(solution)/shard_map/reduce_scatter | solution.py:50
  441.4 1.2 copy-start.12
  441.5 542.0 %reduce-scatter.5.cloned.1.call-start = ((), (), s32[]{:S(2)}) async-start(), calls=%async_computation.12 | async-start | bytes 6488064 | tf_op jit(solution)/shard_map/reduce_scatter | solution.py:48
  576.3 76.3 %copy-start.8 = (bf16[512,1024]{1,0:T(8,128)(2,1)S(1)}, bf16[512,1024]{1,0:T(8,128)(2,1)}, u32[]{:S(2)}) copy-start(bf16[512,1024]{1,0:T(8,128)(2,1)} %fusion.15.n_ref) | copy-start | bytes 3145732
  650.9 1.7 copy-start.10
  658.0 36.3 %copy-start.15 = (f32[1,1024]{1,0:T(1,128)S(1)}, f32[1,1024]{1,0:T(1,128)}, u32[]{:S(2)}) copy-start(f32[1,1024]{1,0:T(1,128)} %copy-done.14) | copy-start | bytes 12292
  658.0 36.3 %copy-start.17 = (f32[512]{0:T(512)S(1)}, f32[512]{0:T(512)}, u32[]{:S(2)}) copy-start(f32[512]{0:T(512)} %copy-done.16) | copy-start | bytes 6148
  658.0 344.3 %all-gather.14.cloned.1.call-start = ((), (), s32[]{:S(2)}) async-start(), calls=%async_computation.15 | async-start | bytes 1679360 | tf_op jit(solution)/shard_map/all_gather | solution.py:54
  694.4 20.7 %copy-start.21 = (f32[512]{0:T(512)S(1)}, f32[512]{0:T(512)}, u32[]{:S(2)}) copy-start(f32[512]{0:T(512)} %copy-done.20) | copy-start | bytes 6148
  694.4 20.7 %copy-start.19 = (f32[512]{0:T(512)S(1)}, f32[512]{0:T(512)}, u32[]{:S(2)}) copy-start(f32[512]{0:T(512)} %copy-done.18) | copy-start | bytes 6148
  763.1 242.3 %copy-start.1 = (bf16[128,5248]{1,0:T(8,128)(2,1)S(1)}, bf16[128,5248]{1,0:T(8,128)(2,1)}, u32[]{:S(2)}) copy-start(bf16[128,5248]{1,0:T(8,128)(2,1)} %param.13) | copy-start | bytes 4030468
Sparse Core Ops, SparseCore 0:
  11.4 72.1 all-gather.5
  87.1 106.7 all-gather.11
  196.8 55.2 all-gather.7
  255.3 96.2 all-gather.9
  410.7 138.1 reduce-scatter.6
  551.1 163.7 reduce-scatter.8
  717.3 149.5 reduce-scatter.10
  872.5 110.9 reduce-scatter.4
  985.0 17.2 all-gather.13

commit v2 on v1

--- a/solution.py
+++ b/solution.py
@@ -29,38 +29,46 @@
     return jax.nn.gelu(pre_act[:, :units], approximate=False) * pre_act[:, units:]
 
 
-def gather_weight(shard):
+def span_groups():
+    size = lax.axis_size("shard")
+    if size == SPAN:
+        return None
+    return [list(range(first, first + SPAN)) for first in range(0, size, SPAN)]
+
+
+def exchange(blocks):
+    return lax.all_to_all(blocks, "shard", 0, 0, tiled=False, axis_index_groups=span_groups())
+
+
+def exchange_all(blocks):
+    return lax.all_to_all(blocks, "shard", 0, 0, tiled=False)
+
+
+def sum_copies(values):
+    size = lax.axis_size("rep")
+    stride = 1
+    while stride < size:
+        pairs = [(i, i ^ stride) for i in range(size)]
+        values = values.astype(jnp.bfloat16)
+        other = lax.ppermute(values, "rep", pairs)
+        values = values.astype(jnp.float32) + other.astype(jnp.float32)
+        stride *= 2
+    return values
+
+
+def sum_copies_wide(values):
+    size = lax.axis_size("rep")
+    stride = 1
+    while stride < size:
+        values = values + lax.ppermute(values, "rep", [(i, i ^ stride) for i in range(size)])
+        stride *= 2
+    return values
+
+
+def copy_part(shard):
     copies = lax.axis_size("rep")
-    mine = lax.axis_index("rep")
-    rows, cols = shard.shape
-    if rows % (8 * copies) == 0:
-        part = lax.dynamic_slice_in_dim(shard, mine * (rows // copies), rows // copies)
-        return lax.all_gather(part, BOTH, axis=0, tiled=True)
-    flat = shard.reshape(rows * cols // 128, 128)
-    count = flat.shape[0] // copies
-    part = lax.dynamic_slice_in_dim(flat, mine * count, count)
-    return lax.all_gather(part, BOTH, axis=0, tiled=True).reshape(-1, cols)
-
-
-def scatter_grad(grad, rows):
-    copies = lax.axis_size("rep")
-    if rows % (8 * copies) == 0:
-        return lax.psum_scatter(grad, BOTH, scatter_dimension=0, tiled=True)
-    flat = grad.reshape(-1, 128)
-    return lax.psum_scatter(flat, BOTH, scatter_dimension=0, tiled=True)
-
-
-def finish_grad(share, rows):
-    whole = lax.all_gather(share, "rep", axis=0, tiled=True)
-    return whole.reshape(rows, -1).astype(jnp.float32)
-
-
-def exchange(blocks):
-    size = lax.axis_size("shard")
-    groups = [list(range(first, first + SPAN)) for first in range(0, size, SPAN)]
-    return lax.all_to_all(
-        blocks, "shard", 0, 0, tiled=False, axis_index_groups=groups if size > SPAN else None
-    )
+    count = shard.shape[0] // copies
+    return lax.dynamic_slice_in_dim(shard, lax.axis_index("rep") * count, count)
 
 
 def lanes(shape):
@@ -77,33 +85,33 @@
     return values * cosine + other * sine
 
 
-def project_body(n_ref, wq_ref, wk_ref, wv_ref, cos_ref, sin_ref, out_ref):
-    rows = n_ref[...]
-    for part, w_ref in enumerate((wq_ref, wk_ref, wv_ref)):
-        result = jnp.dot(rows, w_ref[...], preferred_element_type=jnp.float32)
-        for pair in range(result.shape[1] // PAIR):
-            piece = result[:, pair * PAIR : (pair + 1) * PAIR]
-            if part < 2:
-                piece = turned(piece, cos_ref[...], sin_ref[...])
-            out_ref[pair, :, part * PAIR : (part + 1) * PAIR] = piece.astype(jnp.bfloat16)
-
-
-def project(normed, weight, cosine, sine):
-    rows, width = normed.shape
-    step = 2
-    steps = SPAN // step
-    w_spec = lambda part: pl.BlockSpec(
-        (width, step * PAIR), lambda d: (0, part * steps + d)
-    )
-    whole = lambda array: pl.BlockSpec(array.shape, lambda d: (0, 0))
+def project_body(x_ref, gain_ref, w_ref, cos_ref, sin_ref, out_ref, n_ref):
+    normed = norm_rows(x_ref[...].astype(jnp.float32), gain_ref[0:1, :]).astype(jnp.bfloat16)
+    n_ref[...] = normed
+    result = jnp.dot(normed, w_ref[...], preferred_element_type=jnp.float32)
+    for part in range(3):
+        piece = result[:, part * PAIR : (part + 1) * PAIR]
+        if part < 2:
+            piece = turned(piece, cos_ref[...], sin_ref[...])
+        out_ref[:, part * PAIR : (part + 1) * PAIR] = piece.astype(jnp.bfloat16)
+
+
+def project(tokens, gain, weight, cosine, sine):
+    length, width = tokens.shape
+    step = 512
+    by_rows = lambda columns: pl.BlockSpec((step, columns), lambda i: (i, 0))
+    whole = lambda array: pl.BlockSpec(array.shape, lambda i: (0, 0))
     return pl.pallas_call(
         project_body,
-        grid=(steps,),
-        in_specs=[whole(normed), w_spec(0), w_spec(1), w_spec(2), whole(cosine), whole(sine)],
-        out_specs=pl.BlockSpec((step, rows, 3 * PAIR), lambda d: (d, 0, 0)),
-        out_shape=jax.ShapeDtypeStruct((SPAN, rows, 3 * PAIR), jnp.bfloat16),
+        grid=(length // step,),
+        in_specs=[by_rows(width), whole(gain), whole(weight), by_rows(PAIR), by_rows(PAIR)],
+        out_specs=[by_rows(3 * PAIR), by_rows(width)],
+        out_shape=[
+            jax.ShapeDtypeStruct((length, 3 * PAIR), jnp.bfloat16),
+            jax.ShapeDtypeStruct((length, width), jnp.bfloat16),
+        ],
         name="project_heads",
-    )(normed, weight, weight, weight, cosine, sine)
+    )(tokens, gain, weight, cosine, sine)
 
 
 def nt_dot(a, b):
@@ -275,19 +283,33 @@
     f32, bf16 = jnp.float32, jnp.bfloat16
     rows, width = tokens.shape
     length = SPAN * rows
+    shards = lax.axis_size("shard")
     position = lax.axis_index("shard")
     offset = position % SPAN
-
-    full_qkv = gather_weight(w_qkv)
+    units = w_in.shape[1] // 2
+
+    all_tokens = lax.all_gather(
+        tokens, "shard", axis=0, tiled=True, axis_index_groups=span_groups()
+    )
+    shard_rows = w_qkv.shape[0]
+    by_pair = w_qkv.reshape(shard_rows, 3, SPAN, PAIR).transpose(2, 0, 1, 3)
+    by_pair = by_pair.reshape(SPAN, shard_rows, 3 * PAIR)
+    own_qkv = exchange_all(jnp.concatenate([by_pair] * (shards // SPAN), 0))
+    own_qkv = own_qkv.reshape(width, 3 * PAIR)
     placed = jnp.zeros((2, width), f32)
+    gain_rows = attn_gain.shape[0]
     placed = lax.dynamic_update_slice(
-        placed, jnp.stack([attn_gain, ffn_gain]).astype(f32), (0, position * attn_gain.shape[0])
+        placed, jnp.stack([attn_gain, ffn_gain]).astype(f32), (0, position * gain_rows)
     )
     gains = lax.psum(placed, "shard")
     gain_one, gain_two = gains[0], gains[1]
-    full_out = gather_weight(w_out)
-    full_in = gather_weight(w_in)
-    full_down = gather_weight(w_down)
+    flat_down = w_down.reshape(shard_rows, -1)
+    wide = copy_part(jnp.concatenate([w_in, w_out, flat_down], axis=1))
+    full = lax.all_gather(wide, BOTH, axis=0, tiled=True)
+    full_in = full[:, : 2 * units]
+    full_out = full[:, 2 * units : 2 * units + width]
+    full_down = full[:, 2 * units + width :].reshape(units, width)
+    full_qkv = lax.all_gather(copy_part(w_qkv), BOTH, axis=0, tiled=True)
 
     lane = jnp.arange(PAIR, dtype=jnp.int32)
     half = HEAD_DIM // 2
@@ -295,9 +317,6 @@
     angles = jnp.arange(length, dtype=jnp.int32).astype(f32)[:, None] * frequency[None, :]
     cosine = jnp.cos(angles)
     sine = jnp.sin(angles) * jnp.where(lane % HEAD_DIM < half, -1.0, 1.0)
-    here = offset * rows
-    cosine_here = lax.dynamic_slice_in_dim(cosine, here, rows)
-    sine_here = lax.dynamic_slice_in_dim(sine, here, rows)
     segments = lax.dynamic_slice_in_dim(seg_ids, (position - offset) * rows, length)
     seg_col = jnp.broadcast_to(segments[:, None], (length, 128))
     seg_row = jnp.broadcast_to(segments[None, :], (8, length))
@@ -305,14 +324,12 @@
     lows = jnp.sum(segments[None, :] < firsts[:, None], axis=1, dtype=jnp.int32) // BLOCK
     highs = (jnp.sum(segments[None, :] <= lasts[:, None], axis=1, dtype=jnp.int32) + BLOCK - 1) // BLOCK
 
-    resid_in = tokens.astype(f32)
-    normed_one = norm_rows(resid_in, gain_one).astype(bf16)
-    sent = project(normed_one, full_qkv, cosine_here, sine_here)
-    qkv = exchange(sent).reshape(length, 3 * PAIR)
+    qkv, all_normed = project(all_tokens, jnp.broadcast_to(gain_one, (8, width)), own_qkv, cosine, sine)
     out_heads, lse = attend(qkv, lows, highs, seg_col, seg_row)
     attn_low = jnp.transpose(
         exchange(out_heads.reshape(SPAN, rows, PAIR)), (1, 0, 2)
     ).reshape(rows, width)
+    resid_in = tokens.astype(f32)
     resid_mid = resid_in + jnp.dot(attn_low, full_out, preferred_element_type=f32)
 
     normed_two = norm_rows(resid_mid, gain_two).astype(bf16)
@@ -335,32 +352,39 @@
     grad_down = jnp.einsum("tf,td->fd", units_low, cotangent, preferred_element_type=f32).astype(bf16)
     grad_in = jnp.einsum("td,tf->df", normed_two, grad_pre, preferred_element_type=f32).astype(bf16)
     grad_out = jnp.einsum("td,te->de", attn_low, grad_branch_low, preferred_element_type=f32).astype(bf16)
-    share_down = scatter_grad(grad_down, w_down.shape[0])
-    share_in = scatter_grad(grad_in, w_in.shape[0])
-    share_out = scatter_grad(grad_out, w_out.shape[0])
+    grads = jnp.concatenate([grad_in, grad_out, grad_down.reshape(width, units)], axis=1)
+    share = lax.psum_scatter(grads, BOTH, scatter_dimension=0, tiled=True)
 
     slopes = attend_back(qkv, out_heads, grad_heads, lse, lows, highs, seg_col, seg_row, cosine, sine)
     back = exchange(slopes.reshape(SPAN, rows, 3 * PAIR))
+    own_grad = jnp.einsum("td,tf->df", all_normed, slopes, preferred_element_type=f32).astype(bf16)
+    own_grad = exchange_all(own_grad.reshape(shards, shard_rows, 3 * PAIR))
+    own_grad = own_grad.reshape(shards // SPAN, SPAN, shard_rows, 3, PAIR)
+    if shards == SPAN:
+        own_grad = own_grad[0]
+    else:
+        own_grad = jnp.sum(own_grad.astype(f32), axis=0)
+    own_grad = sum_copies(own_grad)
+    grad_qkv = own_grad.transpose(1, 2, 0, 3).reshape(shard_rows, 3 * width).astype(f32)
     grad_proj = jnp.transpose(back.reshape(SPAN, rows, 3, PAIR), (1, 2, 0, 3)).reshape(rows, 3 * width)
-    grad_qkv = jnp.einsum("td,tf->df", normed_one, grad_proj, preferred_element_type=f32).astype(bf16)
-    share_qkv = scatter_grad(grad_qkv, w_qkv.shape[0])
     grad_normed_one = jnp.einsum("tf,df->td", grad_proj, full_qkv, preferred_element_type=f32).astype(bf16)
     pull_norm_one = jax.vjp(norm_rows, resid_in, gain_one)[1]
     grad_in_norm, grad_gain_one = pull_norm_one(grad_normed_one.astype(f32))
     grad_tokens = (grad_resid + grad_in_norm).astype(bf16)
 
-    gain_sums = lax.psum(jnp.stack([grad_gain_one, grad_gain_two]), BOTH)
-    gain_rows = attn_gain.shape[0]
-    gain_sums = lax.dynamic_slice_in_dim(gain_sums, position * gain_rows, gain_rows, axis=1)
+    gain_parts = jnp.stack([grad_gain_one, grad_gain_two]).reshape(2, shards, gain_rows)
+    gain_parts = exchange_all(jnp.transpose(gain_parts, (1, 0, 2)))
+    gain_sums = sum_copies_wide(jnp.sum(gain_parts, axis=0))
+    done = lax.all_gather(share, "rep", axis=0, tiled=True)
     return (
         layer_out,
         grad_tokens,
         gain_sums[0],
         gain_sums[1],
-        finish_grad(share_qkv, w_qkv.shape[0]),
-        finish_grad(share_out, w_out.shape[0]),
-        finish_grad(share_in, w_in.shape[0]),
-        finish_grad(share_down, w_down.shape[0]),
+        grad_qkv,
+        done[:, 2 * units : 2 * units + width].astype(f32),
+        done[:, : 2 * units].astype(f32),
+        done[:, 2 * units + width :].reshape(w_down.shape).astype(f32),
     )
 
 

time: 1030 us -> 809 us (0.79); the launches traced: 1010 us -> 808 us
  waiting for transfers between devices: 416 us -> 252 us
  blocking collectives: 219 us -> 127 us
  starting transfers between devices: 8.98 us -> 35.5 us
  other arithmetic: 28.7 us -> 48.9 us
  local copies, waits for them, and re-layouts: 47.6 us -> 60.6 us
  Pallas kernels: 179 us -> 167 us
    reduce_scatter x4 -> x1, waiting for transfers between devices: 222 us -> 32.6 us  [local(): share = lax.psum_scatter(grads, BOTH, scatter_dimension=0, tiled=True)]
    all_gather x5 -> x4, waiting for transfers between devices: 95.7 us -> 152 us  [the longest x1 80.7 us: local(): lax.all_gather(tokens, 'shard', axis=0, tiled=True, axis_index_groups=spa...]
    psum x1 -> x0, blocking collectives: 46.3 us -> none  [local(): gain_sums = lax.psum(jnp.stack([grad_gain_one, grad_gain_two]), BOTH)]
    all_gather x3 -> x0, blocking collectives: 43.2 us -> none  [finish_grad(): whole = lax.all_gather(share, 'rep', axis=0, tiled=True)]
    all_to_all x2 -> x4, waiting for transfers between devices: 98.8 us -> 65.6 us  [the longest x1 45.3 us: exchange(): lax.all_to_all(blocks, 'shard', 0, 0, tiled=False, axis_index_groups=span...]
    all_to_all x2 -> x4, starting transfers between devices: 8.14 us -> 34.3 us  [the longest x3 24.9 us: exchange_all(): return lax.all_to_all(blocks, 'shard', 0, 0, tiled=False)]
    all_to_all x2, blocking collectives: 107 us -> 87 us  [exchange(): lax.all_to_all(blocks, 'shard', 0, 0, tiled=False, axis_index_groups=span...]
    psum x1, blocking collectives: 23.4 us -> 40.4 us  [local(): gains = lax.psum(placed, 'shard')]
  transfers between devices with their start and end apart: 11 -> 13, of which waited for: 8 -> 8; matrix products, arithmetic and copies ran while one was open for 10% -> 10% of each run, Pallas kernels for 18% -> 21%
where the time goes in v2:
time: 809 us; the launch traced here: 808 us
  waiting for transfers between devices  252 us (31%)
  Pallas kernels  167 us (21%)
  blocking collectives  127 us (16%)
  matrix products  102 us (13%)
  local copies, waits for them, and re-layouts  60.6 us (7%)
  other arithmetic  48.9 us (6%)
  starting transfers between devices  35.5 us (4%)
  between operations  14.3 us (2%)
    all_to_all x2, blocking collectives, exchange(): lax.all_to_all(blocks, 'shard', 0, 0, tiled=False, axis_index_groups=span...  87 us
    pallas_call x1, Pallas kernels, attend_back(): pl.pallas_call(attend_back_body, in_specs=[spec_smem(), spec_smem()] + [s...  84.3 us
    all_gather x1, waiting for transfers between devices, local(): lax.all_gather(tokens, 'shard', axis=0, tiled=True, axis_index_groups=spa...  80.7 us
    pallas_call x1, Pallas kernels, attend(): pl.pallas_call(attend_body, in_specs=[spec_smem(), spec_smem()] + [spec_v...  69.1 us
    all_gather x1, waiting for transfers between devices, local(): full_qkv = lax.all_gather(copy_part(w_qkv), BOTH, axis=0, tiled=True)  67.9 us
    all_to_all x1, waiting for transfers between devices, exchange(): lax.all_to_all(blocks, 'shard', 0, 0, tiled=False, axis_index_groups=span...  45.3 us
    psum x1, blocking collectives, local(): gains = lax.psum(placed, 'shard')  40.4 us
    reduce_scatter x1, waiting for transfers between devices, local(): share = lax.psum_scatter(grads, BOTH, scatter_dimension=0, tiled=True)  32.6 us
  transfers between devices with their start and end apart: 13, of which 8 were waited for; matrix products, arithmetic and copies ran while one was open for 10% of the time, Pallas kernels for 21%

profile of v2, /device:TPU:0, one launch (start us, length us, event | category | flops | bytes accessed | tf_op | source)
XLA Modules:
  0.0 807.7 jit_solution(8516166632667475163)
XLA Ops:
  7.3 0.7 all-gather.5.cloned.1.call-update
  8.0 2.2 reshape.160
  10.2 1.8 fusion.42
  12.4 0.9 copy.68
  13.4 7.3 all-to-all-start
  21.8 40.4 %psum.7 = f32[2,1024]{1,0:T(2,128)S(1)} all-reduce(f32[2,1024]{1,0:T(2,128)S(1)} %constant_dynamic-update-slice_fusion), channel_id=1, replica_groups=mesh['rep'=4,'shard'=8] {'shard'}, use_global_device_ids=true, to_apply=%region_2.3 | all-reduce | flops 2048 | bytes 16384 | tf_op jit(solution)/shard_map/psum | solution.py:304
  62.2 9.4 %fusion.21 = (f32[4096,128]{1,0:T(8,128)}, f32[4096,128]{1,0:T(8,128)}) fusion(f32[128]{0:T(128)S(1)} %get-tuple-element.77, f32[128]{0:T(128)S(1)} %get-tuple-element.78, f32[4096]{0:T(1024)S(1)} %iota_convert_fusion), kind=kLoop, calls=%fused_computation.54 | loop fusion | flops 1048576 | bytes 4211712 | tf_op jit(solution)/shard_map/mul | solution.py:319
  71.6 1.2 copy.69
  72.8 80.7 %all-gather.5.cloned.1.call-done.x_ref = bf16[4096,1024]{1,0:T(8,128)(2,1)} async-done(((bf16[512,1024]{1,0:T(8,128)(2,1)}), bf16[4096,1024]{1,0:T(8,128)(2,1)}) %all-gather.5.cloned.1.call-update) | async-done | bytes 8388624 | tf_op jit(solution)/shard_map/all_gather | solution.py:291
  153.5 0.6 broadcast_in_dim.25.gain_ref
  154.1 14.0 %project_heads.1 = (bf16[4096,384]{1,0:T(8,128)(2,1)}, bf16[4096,1024]{1,0:T(8,128)(2,1)}) custom-call(bf16[4096,1024]{1,0:T(8,128)(2,1)} %all-gather.5.cloned.1.call-done.x_ref, f32[8,1024]{1,0:T(8,128)} %broadcast_in_dim.25.gain_ref, bf16[1024,384]{1,0:T(8,128)(2,1)} %bitcast.66, f32[4096,128]{1,0:T(8,128)} %get-tuple-element.63.cos_ref, ...), custom_call_target="tpu_custom_call" | custom-call | tf_op jit(solution)/shard_map/project_heads/pallas_call | solution.py:104
  168.1 2.9 broadcast_in_dim.28.segc_ref
  171.1 0.7 broadcast_in_dim.29.segr_ref
  171.7 69.1 %attend_forward.1 = (bf16[4096,128]{1,0:T(8,128)(2,1)}, f32[8,4096]{1,0:T(8,128)}) custom-call(s32[16]{0:T(128)} %get-tuple-element.76.lo_ref, s32[16]{0:T(128)} %get-tuple-element.75.hi_ref, bf16[4096,384]{1,0:T(8,128)(2,1)} %get-tuple-element.12.qkv_ref, s32[4096,128]{1,0:T(8,128)} %broadcast_in_dim.28.segc_ref, s32[8,4096]{1,0:T(8,128)} %broadcast_in_dim.29.segr_ref), custom_call_target="tpu_custom_call" | custom-call | tf_op jit(solution)/shard_map/attend_forward/pallas_call | solution.py:181
  240.9 1.5 copy.70
  242.3 51.5 %all_to_all.30 = bf16[8,512,128]{1,2,0:T(8,128)(2,1)} all-to-all(bf16[8,512,128]{1,2,0:T(8,128)(2,1)S(1)} %copy.70), channel_id=1, replica_groups=mesh['rep'=4,'shard'=8] {'shard'}, dimensions={0} | all-to-all | bytes 2097152 | tf_op jit(solution)/shard_map/all_to_all | solution.py:40
  293.9 3.2 all-gather.7.cloned.1.call-done
  297.0 3.3 fusion.54
  300.7 5.7 slice.64
  306.4 11.3 %reshape.161 = bf16[2624,1024]{1,0:T(8,128)(2,1)} reshape(bf16[1024,2624]{1,0:T(8,128)(2,1)} %slice.64) | data formatting | bytes 10747904 | tf_op jit(solution)/shard_map/reshape | solution.py:311
  317.8 15.6 %fusion.2 = f32[512,5248]{0,1:T(8,128)} fusion(bf16[1024,8896]{1,0:T(8,128)(2,1)} %all-gather.7.cloned.1.call-done, f32[512,1024]{1,0:T(8,128)S(1)} %get-tuple-element.71, f32[1024]{0:T(1024)S(1)} %bitcast.77, f32[512]{0:T(512)S(1)} %fusion.43, f32[512]{0:T(512)S(1)} %broadcast_multiply_fusion.1), kind=kOutput, calls=%fused_computation.5 | convolution fusion | flops 5505024000 | bytes 23601152 | tf_op jit(solution)/shard_map/dot_general | solution.py:336
  333.4 16.8 %bitcast_multiply_fusion.1 = (f32[512,2624]{0,1:T(8,128)}, f32[512,2624]{0,1:T(8,128)S(1)}, bf16[2624,512]{1,0:T(8,128)(2,1)S(1)}) fusion(f32[512,5248]{0,1:T(8,128)} %fusion.2, bf16[2624,1024]{1,0:T(8,128)(2,1)S(1)} %copy-done.3, bf16[512,1024]{1,0:T(8,128)(2,1)} %param.17), kind=kOutput, calls=%fused_computation.11 | convolution fusion | flops 2841477120 | bytes 25231360 | tf_op jit(solution)/shard_map/td,fd->tf/dot_general | solution.py:340
  350.2 5.4 multiply_add_fusion
  355.5 13.1 %convolution_convert_fusion = bf16[1024,5248]{1,0:T(8,128)(2,1)} fusion(f32[512,2624]{0,1:T(8,128)} %get-tuple-element.60, f32[512,2624]{0,1:T(8,128)} %get-tuple-element.58, f32[512,1024]{1,0:T(8,128)S(1)} %get-tuple-element.71, f32[1024]{0:T(1024)S(1)} %bitcast.78, f32[512]{0:T(512)S(1)} %fusion.43, f32[512]{0:T(512)S(1)} %broadcast_multiply_fusion.1), kind=kOutput, calls=%fused_computation.1 | convolution fusion | flops 5515771904 | bytes 23601152 | tf_op jit(solution)/shard_map/td,tf->df/dot_general | solution.py:353
  368.7 14.4 %fusion.19 = (f32[1024]{0:T(1024)S(1)}, f32[512]{0:T(512)S(1)}, bf16[512,1024]{1,0:T(8,128)(2,1)}) fusion(f32[512,1024]{1,0:T(8,128)S(1)} %get-tuple-element.71, f32[512]{0:T(512)S(1)} %fusion.43, f32[512]{0:T(512)S(1)} %broadcast_multiply_fusion.1, f32[1024]{0:T(1024)S(1)} %bitcast.79, bf16[1024,8896]{1,0:T(8,128)(2,1)} %all-gather.7.cloned.1.call-done, ...), kind=kOutput, calls=%fused_computation.52 | convolution fusion | flops 5513017856 | bytes 24655872 | tf_op jit(solution)/shard_map/tf,df->td/dot_general | solution.py:343
  383.0 2.6 fusion.51
  385.6 7.3 convolution_convert_fusion.1
  392.9 11.7 %reshape.169 = bf16[1024,2624]{1,0:T(8,128)(2,1)} reshape(bf16[2624,1024]{1,0:T(8,128)(2,1)} %convolution_convert_fusion.1) | data formatting | bytes 10747904 | tf_op jit(solution)/shard_map/reshape | solution.py:355
  404.6 1.7 fusion.40
  406.3 1.0 copy-done.6
  407.2 2.6 convolution_convert_fusion.3
  409.9 11.6 %pad_maximum_fusion = bf16[1024,8896]{1,0:T(8,128)(2,1)} fusion(bf16[1024,2624]{1,0:T(8,128)(2,1)S(1)} %bitcast.60, bf16[1024,1024]{1,0:T(8,128)(2,1)S(1)} %convolution_convert_fusion.3, bf16[1024,5248]{1,0:T(8,128)(2,1)} %convolution_convert_fusion), kind=kLoop, calls=%fused_computation | loop fusion | flops 54657024 | bytes 36438016 | tf_op jit(solution)/shard_map/concatenate | solution.py:355
  421.7 1.6 constant_dynamic-slice_fusion
  423.4 3.2 fusion.36
  426.8 35.4 %all_to_all.31 = bf16[8,512,128]{2,1,0:T(8,128)(2,1)} all-to-all(bf16[8,512,128]{2,1,0:T(8,128)(2,1)S(1)} %bitcast.65), channel_id=1, replica_groups=mesh['rep'=4,'shard'=8] {'shard'}, dimensions={0} | all-to-all | bytes 2097152 | tf_op jit(solution)/shard_map/all_to_all | solution.py:40
  462.2 84.3 %attend_backward.1 = bf16[4096,384]{1,0:T(8,128)(2,1)} custom-call(s32[16]{0:T(128)} %get-tuple-element.76.lo_ref, s32[16]{0:T(128)} %get-tuple-element.75.hi_ref, bf16[4096,384]{1,0:T(8,128)(2,1)} %get-tuple-element.12.qkv_ref, bf16[4096,128]{1,0:T(8,128)(2,1)} %get-tuple-element.13.out_ref, bf16[4096,128]{1,0:T(8,128)(2,1)} %bitcast.64, ...), custom_call_target="tpu_custom_call" | custom-call | tf_op jit(solution)/shard_map/attend_backward/pallas_call | solution.py:267
  546.6 9.8 %convolution_convert_fusion.5 = bf16[1024,384]{1,0:T(8,128)(2,1)} fusion(bf16[4096,1024]{1,0:T(8,128)(2,1)} %get-tuple-element.15, bf16[4096,384]{1,0:T(8,128)(2,1)} %attend_backward.1), kind=kOutput, calls=%fused_computation.72 | convolution fusion | flops 3221618688 | bytes 12320768 | tf_op jit(solution)/shard_map/td,tf->df/dot_general | solution.py:360
  556.4 2.3 copy.76
  558.6 13.6 %all-to-all-start.5 = ((bf16[8,128,384]{1,2,0:T(8,128)(2,1)}), bf16[8,128,384]{1,2,0:T(8,128)(2,1)}, u32[]{:S(2)}, u32[]{:S(2)}) async-start(bf16[8,128,384]{1,2,0:T(8,128)(2,1)} %copy.76), calls=%async_computation.5 | async-start | bytes 1572864 | tf_op jit(solution)/shard_map/all_to_all | solution.py:44
  572.2 4.7 copy.74
  576.9 19.6 %all-to-all-done.5 = bf16[8,128,384]{1,2,0:T(8,128)(2,1)} async-done(((bf16[8,128,384]{1,2,0:T(8,128)(2,1)}), bf16[8,128,384]{1,2,0:T(8,128)(2,1)}, u32[]{:S(2)}, u32[]{:S(2)}) %all-to-all-start.5) | async-done | bytes 786464 | tf_op jit(solution)/shard_map/all_to_all | solution.py:44
  596.5 9.3 %all-to-all-start.3 = ((bf16[8,512,384]{1,2,0:T(8,128)(2,1)}), bf16[8,512,384]{1,2,0:T(8,128)(2,1)}, u32[]{:S(2)}, u32[]{:S(2)}) async-start(bf16[8,512,384]{1,2,0:T(8,128)(2,1)} %copy.74), calls=%async_computation.3 | async-start | bytes 6291456 | tf_op jit(solution)/shard_map/all_to_all | solution.py:40
  606.2 32.6 %reduce-scatter.2.cloned.1.call-done = bf16[32,8896]{1,0:T(8,128)(2,1)} async-done(((bf16[1024,8896]{1,0:T(8,128)(2,1)}), bf16[32,8896]{1,0:T(8,128)(2,1)}) %reduce-scatter.2.cloned.1.call-update) | async-done | bytes 569360 | tf_op jit(solution)/shard_map/reduce_scatter | solution.py:356
  638.7 8.1 %add_convert_fusion.2 = bf16[512,1024]{1,0:T(8,128)(2,1)} fusion(f32[512,1024]{1,0:T(8,128)} %copy-done.2, bf16[512,2624]{0,1:T(8,128)(2,1)} %get-tuple-element.61, bf16[2624,1024]{1,0:T(8,128)(2,1)} %reshape.161), kind=kOutput, calls=%fused_computation.59 | convolution fusion | flops 2752512000 | bytes 11206656 | tf_op jit(solution)/shard_map/dot_general | solution.py:338
  646.8 2.5 add_convert_fusion.3
  649.4 45.3 %all-to-all-done.3 = bf16[8,512,384]{1,2,0:T(8,128)(2,1)} async-done(((bf16[8,512,384]{1,2,0:T(8,128)(2,1)}), bf16[8,512,384]{1,2,0:T(8,128)(2,1)}, u32[]{:S(2)}, u32[]{:S(2)}) %all-to-all-start.3) | async-done | bytes 3145760 | tf_op jit(solution)/shard_map/all_to_all | solution.py:40
  694.7 3.8 copy.75
  698.5 67.9 %all-gather.9.cloned.1.call-done = bf16[1024,3072]{1,0:T(8,128)(2,1)} async-done(((bf16[32,3072]{1,0:T(8,128)(2,1)}), bf16[1024,3072]{1,0:T(8,128)(2,1)}) %all-gather.9.cloned.1.call-update) | async-done | bytes 6291472 | tf_op jit(solution)/shard_map/all_gather | solution.py:312
  766.4 7.7 fusion.22
  774.1 0.9 copy-done.4
  775.0 1.2 fusion.20
  776.3 0.6 maximum_bitcast_fusion
  776.9 4.1 all-to-all-start.4
  780.9 1.6 add_bitcast_fusion
  782.5 1.2 copy.77
  783.8 3.0 copy.79
  786.8 0.6 all-to-all-done.4
  787.5 1.1 collective-permute-done
  788.7 0.7 collective-permute-start.1
  789.4 3.1 add_convert_fusion.1
  793.0 1.2 slice_convert_fusion.1
  794.2 2.0 reshape.170
  796.1 1.8 slice_convert_fusion.2
  797.9 3.0 slice_convert_fusion
  (68 shorter events, 3.4 us)
Async XLA Ops:
  7.2 4.9 copy-start.5
  7.2 13.6 %copy-start.7 = (s32[4096]{0:T(1024)S(1)}, s32[4096]{0:T(1024)}, u32[]{:S(2)}) copy-start(s32[4096]{0:T(1024)} %param.10) | copy-start | bytes 49156
  7.2 14.5 %copy-start.10 = (bf16[128]{0:T(256)(128)(2,1)S(1)}, bf16[128]{0:T(256)(128)(2,1)}, u32[]{:S(2)}) copy-start(bf16[128]{0:T(256)(128)(2,1)} %param.16) | copy-start | bytes 772
  7.2 14.5 %copy-start.11 = (bf16[128]{0:T(256)(128)(2,1)S(1)}, bf16[128]{0:T(256)(128)(2,1)}, u32[]{:S(2)}) copy-start(bf16[128]{0:T(256)(128)(2,1)} %param.15) | copy-start | bytes 772
  7.2 146.3 %all-gather.5.cloned.1.call-start = ((), (), s32[]{:S(2)}) async-start(), calls=%async_computation.7 | async-start | bytes 9437184 | tf_op jit(solution)/shard_map/all_gather | solution.py:291
  7.9 289.1 %all-gather.7.cloned.1.call-start = ((), (), s32[]{:S(2)}) async-start(), calls=%async_computation.8 | async-start | bytes 18923520 | tf_op jit(solution)/shard_map/all_gather | solution.py:308
  13.4 58.2 %all-to-all-start = ((bf16[8,128,384]{1,2,0:T(8,128)(2,1)}), bf16[8,128,384]{1,2,0:T(8,128)(2,1)S(1)}, u32[]{:S(2)}, u32[]{:S(2)}) async-start(bf16[8,128,384]{1,2,0:T(8,128)(2,1)} %bitcast.5), calls=%async_computation | async-start | bytes 1572864 | tf_op jit(solution)/shard_map/all_to_all | solution.py:44
  20.7 618.0 %reduce-scatter.2.cloned.1.call-start = ((), (), s32[]{:S(2)}) async-start(), calls=%async_computation.10 | async-start | bytes 18923520 | tf_op jit(solution)/shard_map/reduce_scatter | solution.py:356
  62.2 105.9 %copy-start.8 = (f32[1,1024]{1,0:T(1,128)}, f32[1,1024]{1,0:T(1,128)S(1)}, u32[]{:S(2)}) copy-start(f32[1,1024]{1,0:T(1,128)S(1)} %get-tuple-element.65) | copy-start | bytes 12292
  171.1 126.0 %copy-start = (bf16[512,1024]{1,0:T(8,128)(2,1)S(1)}, bf16[512,1024]{1,0:T(8,128)(2,1)}, u32[]{:S(2)}) copy-start(bf16[512,1024]{1,0:T(8,128)(2,1)} %param.9) | copy-start | bytes 3145732
  300.3 68.3 %copy-start.2 = (f32[512,1024]{1,0:T(8,128)}, f32[512,1024]{1,0:T(8,128)S(1)}, u32[]{:S(2)}) copy-start(f32[512,1024]{1,0:T(8,128)S(1)} %get-tuple-element.71) | copy-start | bytes 6291460
  317.8 15.7 %copy-start.3 = (bf16[2624,1024]{1,0:T(8,128)(2,1)S(1)}, bf16[2624,1024]{1,0:T(8,128)(2,1)}, u32[]{:S(2)}) copy-start(bf16[2624,1024]{1,0:T(8,128)(2,1)} %reshape.161) | copy-start | bytes 16121860
  333.4 16.8 %copy-start.1 = (f32[512,5248]{0,1:T(8,128)S(1)}, f32[512,5248]{0,1:T(8,128)}, u32[]{:S(2)}) copy-start(f32[512,5248]{0,1:T(8,128)} %fusion.2) | copy-start | bytes 32243716
  404.6 5.3 slice-start
  406.3 1.0 copy-start.6
  407.2 2.6 slice-start.1
  421.5 344.9 %all-gather.9.cloned.1.call-start = ((), (), s32[]{:S(2)}) async-start(), calls=%async_computation.9 | async-start | bytes 6488064 | tf_op jit(solution)/shard_map/all_gather | solution.py:312
  558.6 37.8 %all-to-all-start.5 = ((bf16[8,128,384]{1,2,0:T(8,128)(2,1)}), bf16[8,128,384]{1,2,0:T(8,128)(2,1)}, u32[]{:S(2)}, u32[]{:S(2)}) async-start(bf16[8,128,384]{1,2,0:T(8,128)(2,1)} %copy.76), calls=%async_computation.5 | async-start | bytes 1572864 | tf_op jit(solution)/shard_map/all_to_all | solution.py:44
  596.5 98.3 %all-to-all-start.3 = ((bf16[8,512,384]{1,2,0:T(8,128)(2,1)}), bf16[8,512,384]{1,2,0:T(8,128)(2,1)}, u32[]{:S(2)}, u32[]{:S(2)}) async-start(bf16[8,512,384]{1,2,0:T(8,128)(2,1)} %copy.74), calls=%async_computation.3 | async-start | bytes 6291456 | tf_op jit(solution)/shard_map/all_to_all | solution.py:40
  605.8 187.1 %all-gather.11.cloned.1.call-start = ((), (), s32[]{:S(2)}) async-start(), calls=%async_computation.11 | async-start | bytes 2867200 | tf_op jit(solution)/shard_map/all_gather | solution.py:378
  606.1 40.8 %collective-permute-start.2 = (bf16[8,128,3,128]{1,3,2,0:T(8,128)(2,1)}, bf16[8,128,3,128]{1,3,2,0:T(8,128)(2,1)}, u32[]{:S(2)}, u32[]{:S(2)}) collective-permute-start(bf16[8,128,3,128]{1,3,2,0:T(8,128)(2,1)} %bitcast.24), channel_id=1, source_target_pairs={{0,8},{8,0},{16,24},{24,16},{1,9},{9,1},{17,25},{25,17},{2,10},{10... | collective-permute-start | bytes 2359304 | tf_op jit(solution)/shard_map/ppermute | solution.py:53
  646.8 119.6 %copy-start.9 = (f32[1,1024]{1,0:T(1,128)S(1)}, f32[1,1024]{1,0:T(1,128)}, u32[]{:S(2)}) copy-start(f32[1,1024]{1,0:T(1,128)} %copy-done.8) | copy-start | bytes 12292
  649.4 131.5 %collective-permute-start.3 = (bf16[8,128,3,128]{1,3,2,0:T(8,128)(2,1)}, bf16[8,128,3,128]{1,3,2,0:T(8,128)(2,1)}, u32[]{:S(2)}, u32[]{:S(2)}) collective-permute-start(bf16[8,128,3,128]{1,3,2,0:T(8,128)(2,1)} %add_convert_fusion.3), channel_id=1, source_target_pairs={{0,16},{8,24},{16,0},{24,8},{1,17},{9,25},{17,1},{25,9},{2,18},{10... | collective-permute-start | bytes 2359304 | tf_op jit(solution)/shard_map/ppermute | solution.py:53
  774.1 1.0 copy-start.4
  776.9 10.6 %all-to-all-start.4 = ((f32[8,2,128]{2,1,0:T(2,128)}), f32[8,2,128]{2,1,0:T(2,128)S(1)}, u32[]{:S(2)}, u32[]{:S(2)}) async-start(f32[8,2,128]{2,1,0:T(2,128)} %maximum_bitcast_fusion), calls=%async_computation.4 | async-start | bytes 16384 | tf_op jit(solution)/shard_map/all_to_all | solution.py:44
  787.5 1.2 collective-permute-start
  788.7 3.7 collective-permute-start.1
Sparse Core Ops, SparseCore 0:
  10.1 143.2 all-gather.4
  156.9 140.1 all-gather.6
  421.6 217.0 reduce-scatter.1
  642.0 124.3 all-gather.8
  767.8 22.1 all-gather.10
